TPU v7x, 512 devices: a whole 4x4x16 slice. The times are simulated.
512 devices in a mesh: pix: 128 (over z, x_lo, y), batch: 4 (over x_hi, core).
Axes of the slice: x: 4 (x_hi: 2, x_lo: 2; x = x_hi * 2 + x_lo), y: 4, z: 16, core: 2. Of those that a mesh axis runs over, the one named last changes fastest.
Arguments:
- fine_tokens: bfloat16 [524288, 512], P(('batch', 'pix')), parts along dimension 0, may hold values from -8 to 8
- parent_tokens: bfloat16 [131072, 512], P(('batch', 'pix')), parts along dimension 0, may hold values from -8 to 8
- shift_table: int32 [131072], P('pix'), may hold values from 0 to 131071, as said below
- parent_slot: int32 [32768], P('pix'), may hold values from 0 to 255, as said below
- fine_gain: float32 [512], replicated, may hold values from 0.1 to 1.9
- parent_gain: float32 [512], replicated, may hold values from 0.1 to 1.9
- w_qkv: bfloat16 [512, 1536], replicated, may hold values from -2 to 2
- w_parent: bfloat16 [512, 1024], replicated, may hold values from -2 to 2
- w_out: bfloat16 [1024, 512], replicated, may hold values from -0.1875 to 0.1875
Outputs:
- mixed: bfloat16 [524288, 512], P(('batch', 'pix')), parts along dimension 0
There are 4 independent parts, one for each index of `batch`. A program takes and returns all parts, laid end to end along the dimension named above; an argument that names none is the same for every part. Nothing has to cross between parts.
Inputs may be any that keep to these rules, and one draw needn't show every extreme that they name: Every entry shift_table[p] equals (p + o) mod 131072 with -128 <= o <= 128; on every device one entry has o = 128 and one o = -128. Over the stored rows of one owner j, parent_slot takes every value 0 to 255 once.
All inputs are finite; a program needn't handle non-finite values.
Results may differ from a plain program's by a relative error of at most 0.0018.
The roundings to bfloat16 on the way count: a program that leaves them out, or rounds other values in their place, can miss the bound.
Values may be sent and summed in bfloat16 or wider, within the bound.
A program may use at most 64 MiB of HBM per device.

v0:
```python
import jax
import jax.numpy as jnp
from jax import lax
from jax.sharding import PartitionSpec as P

HEADS = 16
WIN = 256
HALO = 128
PWIN = 64


def with_halo(cells, sides, width):
    for axis, dim in sides:
        count = lax.axis_size(axis)
        head = lax.slice_in_dim(cells, 0, width, axis=dim)
        tail = lax.slice_in_dim(cells, cells.shape[dim] - width, cells.shape[dim], axis=dim)
        cells = jnp.concatenate(
            [
                lax.ppermute(tail, axis, [(i, (i + 1) % count) for i in range(count)]),
                cells,
                lax.ppermute(head, axis, [((i + 1) % count, i) for i in range(count)]),
            ],
            axis=dim,
        )
    return cells


def rms_rows(matrix, gain):
    values = matrix.astype(jnp.float32)
    factor = lax.rsqrt(jnp.mean(values * values, axis=-1, keepdims=True) + 1e-06)
    return (values * factor * gain).astype(jnp.bfloat16)


def attend(queries, key_heads, value_heads):
    scores = jnp.einsum("wrhe,wshe->whrs", queries, key_heads, preferred_element_type=jnp.float32)
    scores = scores / jnp.sqrt(jnp.float32(key_heads.shape[-1]))
    highest = jnp.max(scores, axis=-1, keepdims=True)
    powers = jnp.exp(scores - highest)
    weights = (powers / jnp.sum(powers, axis=-1, keepdims=True)).astype(jnp.bfloat16)
    result = jnp.einsum("whrs,wshe->wrhe", weights, value_heads, preferred_element_type=jnp.float32)
    return result.astype(jnp.bfloat16)


def on_device(
    fine_tokens,
    parent_tokens,
    shift_table,
    parent_slot,
    fine_gain,
    parent_gain,
    w_qkv,
    w_parent,
    w_out,
):
    row_count, features = fine_tokens.shape
    devices = lax.axis_size("pix")
    offset_rows = lax.axis_index("pix") * row_count
    all_rows = row_count * devices
    normed = rms_rows(fine_tokens, fine_gain)
    qkv = jnp.dot(normed, w_qkv, preferred_element_type=jnp.float32).astype(jnp.bfloat16)
    extended = with_halo(qkv[:, features:], (("pix", 0),), HALO)
    local_index = jnp.mod(shift_table - offset_rows + HALO, all_rows)
    window_kv = jnp.take(extended, local_index, axis=0)
    arrived, slots = (
        lax.all_to_all(parent_tokens, "pix", split_axis=0, concat_axis=0, tiled=True),
        lax.all_to_all(parent_slot, "pix", split_axis=0, concat_axis=0, tiled=True),
    )
    ordered = jnp.zeros_like(arrived).at[slots].set(arrived)
    parent_kv = jnp.dot(
        rms_rows(ordered, parent_gain), w_parent, preferred_element_type=jnp.float32
    ).astype(jnp.bfloat16)
    head_size = features // HEADS
    windows = row_count // WIN
    queries = qkv[:, :features].reshape(windows, WIN, HEADS, head_size)
    self_keys = window_kv[:, :features].reshape(windows, WIN, HEADS, head_size)
    self_values = window_kv[:, features:].reshape(windows, WIN, HEADS, head_size)
    cross_keys = parent_kv[:, :features].reshape(windows, PWIN, HEADS, head_size)
    cross_values = parent_kv[:, features:].reshape(windows, PWIN, HEADS, head_size)
    self_out = attend(queries, self_keys, self_values).reshape(row_count, features)
    cross_out = attend(queries, cross_keys, cross_values).reshape(row_count, features)
    joined = jnp.concatenate([self_out, cross_out], axis=1)
    branch = jnp.dot(joined, w_out, preferred_element_type=jnp.float32)
    return (fine_tokens.astype(jnp.float32) + branch).astype(jnp.bfloat16)


def solution(mesh):
    return jax.shard_map(
        on_device,
        mesh=mesh,
        in_specs=(
            P(("batch", "pix"), None),
            P(("batch", "pix"), None),
            P("pix"),
            P("pix"),
            P(),
            P(),
            P(),
            P(),
            P(),
        ),
        out_specs=P(("batch", "pix"), None),
        check_vma=False,
    )
```

profile of v0, /device:TPU:4, one launch (start us, length us, event | category | flops | bytes accessed | tf_op | source)
XLA Modules:
  0.0 118.8 jit_solution(9106678738671186229)
XLA Ops:
  0.0 1.6 %fusion.12 = f32[1024]{0:T(1024)S(1)} fusion(bf16[1024,512]{1,0:T(8,128)(2,1)} %param.9), kind=kLoop, calls=%fused_computation.20 | loop fusion | flops 1571840 | bytes 1052672 | tf_op jit(solution)/shard_map/reduce_sum | solution.py:30
  1.7 3.1 %convolution_convert_fusion = bf16[1024,1536]{1,0:T(8,128)(2,1)S(1)} fusion(bf16[512,1536]{1,0:T(8,128)(2,1)S(1)} %copy-done, bf16[1024,512]{1,0:T(8,128)(2,1)} %param.9, f32[512]{0:T(512)} %param.13, f32[1024]{0:T(1024)S(1)} %add_rsqrt_fusion), kind=kOutput, calls=%fused_computation.13 | convolution fusion | flops 1614282752 | bytes 5773312 | tf_op jit(solution)/shard_map/dot_general | solution.py:60
  4.8 1.6 %copy-done.1 = bf16[1024,1536]{1,0:T(8,128)(2,1)} copy-done((bf16[1024,1536]{1,0:T(8,128)(2,1)}, bf16[1024,1536]{1,0:T(8,128)(2,1)S(1)}, u32[]{:S(2)}) %copy-start.1) | copy-done | bytes 3145752
  7.3 3.5 %collective-permute-start = (bf16[128,1024]{1,0:T(8,128)(2,1)}, bf16[128,1024]{1,0:T(8,128)(2,1)S(1)}, u32[]{:S(2)}, u32[]{:S(2)}) collective-permute-start(bf16[128,1024]{1,0:T(8,128)(2,1)} %get-tuple-element.5), channel_id=1, source_target_pairs={{0,4},{4,8},{8,12},{12,16},{16,20},{20,24},{24,28},{28,32},{32,36}... | collective-permute-start | bytes 786440 | tf_op jit(solution)/shard_map/ppermute | solution.py:19
  10.8 12.9 %collective-permute-start.1 = (bf16[128,1024]{1,0:T(8,128)(2,1)}, bf16[128,1024]{1,0:T(8,128)(2,1)S(1)}, u32[]{:S(2)}, u32[]{:S(2)}) collective-permute-start(bf16[128,1024]{1,0:T(8,128)(2,1)} %get-tuple-element.6), channel_id=1, source_target_pairs={{4,0},{8,4},{12,8},{16,12},{20,16},{24,20},{28,24},{32,28},{36,32}... | collective-permute-start | bytes 786440 | tf_op jit(solution)/shard_map/ppermute | solution.py:21
  24.5 11.0 %all-to-all-start = ((s32[128,2,1]{1,2,0:T(1,128)}), s32[128,2,1]{1,2,0:T(1,128)S(1)}, u32[]{:S(2)}, u32[]{:S(2)}) async-start(s32[128,2,1]{1,2,0:T(1,128)} %bitcast.1), calls=%async_computation | async-start | bytes 131072 | tf_op jit(solution)/shard_map/all_to_all | solution.py:66
  35.6 3.2 %slice.37 = bf16[1024,1024]{1,0:T(8,128)(2,1)} slice(bf16[1024,1536]{1,0:T(8,128)(2,1)} %copy-done.1), slice={[0:1024], [512:1536]} | slice | bytes 4194304 | tf_op jit(solution)/shard_map/slice | solution.py:61
  40.1 2.6 %reshape.81 = bf16[4,256,16,32]{1,0,3,2:T(4,128)(2,1)} reshape(bf16[1024,512]{0,1:T(8,128)(2,1)} %copy.45) | data formatting | bytes 2097152 | tf_op jit(solution)/shard_map/reshape | solution.py:74
  43.6 6.6 %all-to-all-done = s32[128,2,1]{1,2,0:T(1,128)S(1)} async-done(((s32[128,2,1]{1,2,0:T(1,128)}), s32[128,2,1]{1,2,0:T(1,128)S(1)}, u32[]{:S(2)}, u32[]{:S(2)}) %all-to-all-start) | async-done | bytes 1056 | tf_op jit(solution)/shard_map/all_to_all | solution.py:66
  50.1 10.6 %all-to-all-start.1 = ((bf16[128,2,512]{2,1,0:T(2,128)(2,1)}), bf16[128,2,512]{2,1,0:T(2,128)(2,1)S(1)}, u32[]{:S(2)}, u32[]{:S(2)}) async-start(bf16[128,2,512]{2,1,0:T(2,128)(2,1)} %all_to_all.19), calls=%async_computation.1 | async-start | bytes 524288 | tf_op jit(solution)/shard_map/all_to_all | solution.py:65
  62.3 3.3 %pad_maximum_fusion = bf16[1280,1024]{1,0:T(8,128)(2,1)} fusion(bf16[128,1024]{1,0:T(8,128)(2,1)S(1)} %collective-permute-done.1, bf16[1024,1024]{1,0:T(8,128)(2,1)} %slice.37, bf16[128,1024]{1,0:T(8,128)(2,1)S(1)} %collective-permute-done), kind=kLoop, calls=%fused_computation.19 | loop fusion | flops 7864320 | bytes 5242880 | tf_op jit(solution)/shard_map/concatenate | solution.py:17
  65.6 8.1 %gather_fusion = bf16[1024,1024]{1,0:T(8,128)(2,1)} fusion(bf16[1280,1024]{1,0:T(8,128)(2,1)} %pad_maximum_fusion, s32[1024]{0:T(1024)S(1)} %broadcast_clamp_fusion), kind=kCustom, calls=%fused_computation | custom fusion | bytes 4198400 | tf_op jit(solution)/shard_map/jit(_take)/gather | solution.py:63
  73.7 1.9 %broadcast_select_fusion = bf16[1024,1024]{1,0:T(8,128)(2,1)S(1)} fusion(bf16[1024,1024]{1,0:T(8,128)(2,1)} %gather_fusion, pred[1024]{0:T(1024)(128)(4,1)S(1)} %compare_and_fusion), kind=kLoop, calls=%fused_computation.30 | loop fusion | flops 1048576 | bytes 4195328 | tf_op jit(solution)/shard_map/jit(_take)/select_n | solution.py:63
  77.1 1.5 %copy.46 = bf16[1024,512]{0,1:T(8,128)(2,1)S(1)} copy(bf16[1024,512]{1,0:T(8,128)(2,1)} %get-tuple-element.8) | data formatting | bytes 2097152 | tf_op jit(solution)/shard_map/slice | solution.py:75
  78.5 1.6 %reshape.82 = bf16[4,256,16,32]{1,0,3,2:T(4,128)(2,1)} reshape(bf16[1024,512]{0,1:T(8,128)(2,1)S(1)} %copy.46) | data formatting | bytes 2097152 | tf_op jit(solution)/shard_map/reshape | solution.py:75
  80.1 1.5 %copy.44 = bf16[1024,512]{0,1:T(8,128)(2,1)S(1)} copy(bf16[1024,512]{1,0:T(8,128)(2,1)} %get-tuple-element.7) | data formatting | bytes 2097152 | tf_op jit(solution)/shard_map/slice | solution.py:76
  81.6 1.6 %reshape.80 = bf16[4,256,16,32]{1,0,3,2:T(4,128)(2,1)} reshape(bf16[1024,512]{0,1:T(8,128)(2,1)S(1)} %copy.44) | data formatting | bytes 2097152 | tf_op jit(solution)/shard_map/reshape | solution.py:76
  83.2 10.4 %fusion.63 = (f32[4,16,256]{2,1,0:T(8,128)S(1)}, f32[4,16,256,256]{2,3,1,0:T(8,128)}) fusion(bf16[4,256,16,32]{1,0,3,2:T(4,128)(2,1)} %reshape.82, bf16[4,256,16,32]{1,0,3,2:T(4,128)(2,1)} %reshape.81), kind=kOutput, calls=%fused_computation.74 | convolution fusion | flops 281018624 | bytes 18939904 | tf_op jit(solution)/shard_map/sub | solution.py:38
  93.6 7.3 %fusion.27 = bf16[4,256,16,32]{1,3,2,0:T(8,128)(2,1)S(1)} fusion(f32[4,16,256,256]{2,3,1,0:T(8,128)} %get-tuple-element.14, f32[4,16,256]{2,1,0:T(8,128)S(1)} %get-tuple-element.13, bf16[4,256,16,32]{1,0,3,2:T(4,128)(2,1)S(1)} %copy-done.5), kind=kOutput, calls=%fused_computation.34 | convolution fusion | flops 277348352 | bytes 18939904 | tf_op jit(solution)/shard_map/whrs,wshe->wrhe/dot_general | solution.py:40
  103.1 1.8 %scatter_custom_fusion = bf16[256,512]{1,0:T(8,128)(2,1)S(1)} fusion(s32[256]{0:T(256)S(1)} %bitcast.34, bf16[256,512]{1,0:T(8,128)(2,1)S(1)} %reshape.99, bf16[]{:T(256)} %constant.60.clone.1), kind=kCustom, calls=%fused_computation.55 | custom fusion | bytes 262146 | tf_op jit(solution)/shard_map/scatter | solution.py:68
  105.0 1.7 %convolution_convert_fusion.1 = bf16[256,1024]{1,0:T(8,128)(2,1)S(1)} fusion(bf16[512,1024]{1,0:T(8,128)(2,1)} %param.16, bf16[256,512]{1,0:T(8,128)(2,1)S(1)} %scatter_custom_fusion, f32[512]{0:T(512)S(1)} %copy-done.9, f32[256]{0:T(256)S(1)} %add_rsqrt_fusion.1), kind=kOutput, calls=%fused_computation.35 | convolution fusion | flops 269221888 | bytes 1838080 | tf_op jit(solution)/shard_map/dot_general | solution.py:69
  108.7 3.0 %fusion.62 = (f32[4,16,256]{2,1,0:T(8,128)S(1)}, f32[4,16,256,64]{2,3,1,0:T(8,128)}) fusion(f32[4,16,256,64]{2,3,1,0:T(8,128)S(1)} %fusion.42), kind=kOutput, calls=%fused_computation.73 | output fusion | flops 4194367 | bytes 8454144 | tf_op jit(solution)/shard_map/sub | solution.py:38
  112.0 2.6 %fusion.26 = bf16[4,256,16,32]{1,3,2,0:T(8,128)(2,1)S(1)} fusion(f32[4,16,256,64]{2,3,1,0:T(8,128)} %get-tuple-element.12, f32[4,16,256]{2,1,0:T(8,128)S(1)} %get-tuple-element.11, bf16[4,64,16,32]{1,0,3,2:T(4,128)(2,1)S(1)} %reshape.84), kind=kOutput, calls=%fused_computation.33 | convolution fusion | flops 69730304 | bytes 5570560 | tf_op jit(solution)/shard_map/whrs,wshe->wrhe/dot_general | solution.py:40
  116.6 2.3 %fusion.15 = bf16[1024,512]{1,0:T(8,128)(2,1)} fusion(bf16[1024,512]{1,0:T(8,128)(2,1)S(1)} %copy-done.3, bf16[1024,512]{1,0:T(8,128)(2,1)S(1)} %copy-done.11, bf16[1024,512]{0,1:T(8,128)(2,1)S(1)} %bitcast.33, bf16[1024,512]{0,1:T(8,128)(2,1)S(1)} %bitcast.32), kind=kOutput, calls=%fused_computation.23 | convolution fusion | flops 1079508992 | bytes 5242880 | tf_op jit(solution)/shard_map/dot_general | solution.py:82
  (53 shorter events, 13.2 us)
Async XLA Ops:
  0.0 1.7 %copy-start = (bf16[512,1536]{1,0:T(8,128)(2,1)S(1)}, bf16[512,1536]{1,0:T(8,128)(2,1)}, u32[]{:S(2)}) copy-start(bf16[512,1536]{1,0:T(8,128)(2,1)} %param.15) | copy-start | bytes 4718596
  1.7 22.0 %copy-start.10 = (s32[256]{0:T(256)S(1)}, s32[256]{0:T(256)}, u32[]{:S(2)}) copy-start(s32[256]{0:T(256)} %param.12) | copy-start | bytes 3076
  1.7 33.8 %copy-start.8 = (s32[1024]{0:T(1024)S(1)}, s32[1024]{0:T(1024)}, u32[]{:S(2)}) copy-start(s32[1024]{0:T(1024)} %param.11) | copy-start | bytes 12292
  4.8 1.7 %copy-start.1 = (bf16[1024,1536]{1,0:T(8,128)(2,1)}, bf16[1024,1536]{1,0:T(8,128)(2,1)S(1)}, u32[]{:S(2)}) copy-start(bf16[1024,1536]{1,0:T(8,128)(2,1)S(1)} %convolution_convert_fusion) | copy-start | bytes 9437188
  7.3 54.9 %collective-permute-start = (bf16[128,1024]{1,0:T(8,128)(2,1)}, bf16[128,1024]{1,0:T(8,128)(2,1)S(1)}, u32[]{:S(2)}, u32[]{:S(2)}) collective-permute-start(bf16[128,1024]{1,0:T(8,128)(2,1)} %get-tuple-element.5), channel_id=1, source_target_pairs={{0,4},{4,8},{8,12},{12,16},{16,20},{20,24},{24,28},{28,32},{32,36}... | collective-permute-start | bytes 786440 | tf_op jit(solution)/shard_map/ppermute | solution.py:19
  10.8 51.4 %collective-permute-start.1 = (bf16[128,1024]{1,0:T(8,128)(2,1)}, bf16[128,1024]{1,0:T(8,128)(2,1)S(1)}, u32[]{:S(2)}, u32[]{:S(2)}) collective-permute-start(bf16[128,1024]{1,0:T(8,128)(2,1)} %get-tuple-element.6), channel_id=1, source_target_pairs={{4,0},{8,4},{12,8},{16,12},{20,16},{24,20},{28,24},{32,28},{36,32}... | collective-permute-start | bytes 786440 | tf_op jit(solution)/shard_map/ppermute | solution.py:21
  24.5 25.6 %all-to-all-start = ((s32[128,2,1]{1,2,0:T(1,128)}), s32[128,2,1]{1,2,0:T(1,128)S(1)}, u32[]{:S(2)}, u32[]{:S(2)}) async-start(s32[128,2,1]{1,2,0:T(1,128)} %bitcast.1), calls=%async_computation | async-start | bytes 131072 | tf_op jit(solution)/shard_map/all_to_all | solution.py:66
  35.6 3.2 %slice-start = ((bf16[1024,1536]{1,0:T(8,128)(2,1)}), bf16[1024,512]{1,0:T(8,128)(2,1)S(1)}, s32[]{:S(2)}) async-start(bf16[1024,1536]{1,0:T(8,128)(2,1)} %copy-done.1), calls=%async_computation.2 | async-start | bytes 2097152 | tf_op jit(solution)/shard_map/slice | solution.py:74
  38.8 4.0 %copy-start.7 = (bf16[256,512]{1,0:T(8,128)(2,1)S(1)}, bf16[256,512]{1,0:T(8,128)(2,1)}, u32[]{:S(2)}) copy-start(bf16[256,512]{1,0:T(8,128)(2,1)} %param.10) | copy-start | bytes 786436
  50.1 52.8 %all-to-all-start.1 = ((bf16[128,2,512]{2,1,0:T(2,128)(2,1)}), bf16[128,2,512]{2,1,0:T(2,128)(2,1)S(1)}, u32[]{:S(2)}, u32[]{:S(2)}) async-start(bf16[128,2,512]{2,1,0:T(2,128)(2,1)} %all_to_all.19), calls=%async_computation.1 | async-start | bytes 524288 | tf_op jit(solution)/shard_map/all_to_all | solution.py:65
  83.2 10.4 %copy-start.5 = (bf16[4,256,16,32]{1,0,3,2:T(4,128)(2,1)S(1)}, bf16[4,256,16,32]{1,0,3,2:T(4,128)(2,1)}, u32[]{:S(2)}) copy-start(bf16[4,256,16,32]{1,0,3,2:T(4,128)(2,1)} %reshape.80) | copy-start | bytes 3145732
  100.9 4.2 %copy-start.9 = (f32[512]{0:T(512)S(1)}, f32[512]{0:T(512)}, u32[]{:S(2)}) copy-start(f32[512]{0:T(512)} %param.14) | copy-start | bytes 6148
  103.0 4.9 %copy-start.2 = (bf16[4,256,16,32]{1,0,3,2:T(4,128)(2,1)S(1)}, bf16[4,256,16,32]{1,0,3,2:T(4,128)(2,1)}, u32[]{:S(2)}) copy-start(bf16[4,256,16,32]{1,0,3,2:T(4,128)(2,1)} %reshape.81) | copy-start | bytes 3145732
  108.7 3.0 %copy-start.6 = (bf16[256,512]{1,0:T(8,128)(2,1)S(1)}, bf16[256,512]{1,0:T(8,128)(2,1)}, u32[]{:S(2)}) copy-start(bf16[256,512]{1,0:T(8,128)(2,1)} %get-tuple-element.9) | copy-start | bytes 786436
  114.7 1.2 %copy-start.3 = (bf16[1024,512]{1,0:T(8,128)(2,1)S(1)}, bf16[1024,512]{1,0:T(8,128)(2,1)}, u32[]{:S(2)}) copy-start(bf16[1024,512]{1,0:T(8,128)(2,1)} %param.9) | copy-start | bytes 3145732
  114.7 1.5 %copy-start.4 = (bf16[64,8,4,256]{3,1,2,0:T(8,128)(2,1)S(1)}, bf16[64,8,4,256]{3,1,2,0:T(8,128)(2,1)}, u32[]{:S(2)}) copy-start(bf16[64,8,4,256]{3,1,2,0:T(8,128)(2,1)} %copy.60) | copy-start | bytes 3145732
  114.7 1.8 %copy-start.11 = (bf16[1024,512]{1,0:T(8,128)(2,1)S(1)}, bf16[1024,512]{1,0:T(8,128)(2,1)}, u32[]{:S(2)}) copy-start(bf16[1024,512]{1,0:T(8,128)(2,1)} %param.17) | copy-start | bytes 3145732
where the time goes:
time: 119 us
  starting transfers between devices  38 us (32%)
  local copies, waits for them, and re-layouts  35 us (29%)
  matrix products  28.1 us (24%)
  other arithmetic  10.8 us (9%)
  waiting for transfers between devices  6.59 us (6%)
    ppermute x1, starting transfers between devices, with_halo(): lax.ppermute(head, axis, [((i + 1) % count, i) for i in range(count)])  12.9 us
    all_to_all x1, starting transfers between devices, on_device(): lax.all_to_all(parent_slot, 'pix', split_axis=0, concat_axis=0, tiled=True)  11 us
    all_to_all x1, starting transfers between devices, on_device(): lax.all_to_all(parent_tokens, 'pix', split_axis=0, concat_axis=0, tiled=T...  10.6 us
    sub x1, matrix products, attend(): powers = jnp.exp(scores - highest)  10.4 us
    dot_general x2, matrix products, attend(): jnp.einsum('whrs,wshe->wrhe', weights, value_heads, preferred_element_typ...  9.93 us
    gather x1, local copies, waits for them, and re-layouts, on_device(): window_kv = jnp.take(extended, local_index, axis=0)  8.13 us
    all_to_all x1, waiting for transfers between devices, on_device(): lax.all_to_all(parent_slot, 'pix', split_axis=0, concat_axis=0, tiled=True)  6.59 us
    unnamed x26, local copies, waits for them, and re-layouts  3.9 us
  transfers between devices with their start and end apart: 4, of which 1 were waited for; matrix products, arithmetic and copies ran while one was open for 41% of the time, Pallas kernels for 0%

commit v1 on v0

v1 whole, which is shorter than its diff:
```python
import functools

import jax
import jax.numpy as jnp
from jax import lax
from jax.experimental import pallas as pl
from jax.experimental.pallas import tpu as pltpu
from jax.sharding import PartitionSpec as P

HEADS = 16
WIN = 256
HALO = 128
PWIN = 64
ZN = 16
XYN = 8
NEAR = (0, 1, 2, 3, 4, 13, 14, 15)
FAR = (8, 7, 9, 6, 10, 5, 11, 12)
MESH = pl.DeviceIdType.MESH
F32 = jnp.float32
BF16 = jnp.bfloat16
SCALE = 1.4426950408889634 / (32.0**0.5)

NN = (((1,), (0,)), ((), ()))
NT = (((1,), (1,)), ((), ()))
TN = (((0,), (0,)), ((), ()))


def dot(a, b, dims=NN):
    return lax.dot_general(a, b, dims, preferred_element_type=F32)


def rms_rows(rows, gain):
    values = rows.astype(F32)
    factor = lax.rsqrt(jnp.mean(values * values, axis=-1, keepdims=True) + 1e-06)
    return (values * factor * gain).astype(BF16)


def softmax_rows(scores):
    powers = jnp.exp2((scores - jnp.max(scores, axis=0, keepdims=True)) * SCALE)
    return (powers * (1.0 / jnp.sum(powers, axis=0, keepdims=True))).astype(BF16)


def kernel(
    fine, par, shift, pslot, fgain, pgain, wqkv, wpar, wout, out,
    xv, ext, halo, qv, kv, vt, ot, acc, relb, shv, fgv, pgv,
    wq, wp, wo, wvt, wpvt, zbuf, tbuf, fbuf, zslot, fslot, kpv, vpt, ov,
    in_sem, out_sem, own_sem, hs_sem, hr_sem, zs_sem, zr_sem, zss_sem, zsr_sem,
    ps_sem, pr_sem, pss_sem, psr_sem,
):
    me = lax.axis_index("pix")
    count = ZN * XYN
    z = me // XYN
    xy = me % XYN
    right = (me + 1) % count
    left = (me + count - 1) % count
    rows = xv.shape[0]
    features = xv.shape[1]
    windows = rows // WIN
    total = rows * count

    loads = [
        pltpu.make_async_copy(fine.at[pl.ds(WIN * i, WIN)], xv.at[pl.ds(WIN * i, WIN)], in_sem.at[i])
        for i in range(4)
    ]
    loads.append(pltpu.make_async_copy(fgain, fgv, in_sem.at[4]))
    loads.append(pltpu.make_async_copy(shift, shv, in_sem.at[5]))
    loads.append(pltpu.make_async_copy(wqkv, wq, in_sem.at[6]))
    loads.append(pltpu.make_async_copy(wpar, wp, in_sem.at[7]))
    loads.append(pltpu.make_async_copy(wout, wo, in_sem.at[8]))
    loads.append(pltpu.make_async_copy(pgain, pgv, in_sem.at[9]))

    barrier = pltpu.get_barrier_semaphore()
    peers = [((z + k) % ZN) * XYN + xy for k in range(1, ZN)]
    peers += [z * XYN + (xy + m) % XYN for m in range(1, XYN)]
    peers += [left, right]
    for peer in peers:
        pl.semaphore_signal(barrier, inc=1, device_id={"pix": peer}, device_id_type=MESH)
    for load in loads:
        load.start()

    loads[4].wait()
    loads[5].wait()
    place = lax.broadcasted_iota(jnp.int32, (8, 128), 0) * 128 + lax.broadcasted_iota(
        jnp.int32, (8, 128), 1
    )
    away = shv[...] - (place + me * rows)
    away = jnp.where(away > total // 2, away - total, away)
    away = jnp.where(away < -(total // 2), away + total, away)
    rel = ((place % WIN) + away + HALO).astype(F32)
    for i in range(8):
        relb[128 * i : 128 * (i + 1), :] = jnp.transpose(
            jnp.broadcast_to(rel[i : i + 1, :], (128, 128))
        )
    gain = fgv[...]
    for i in range(4):
        loads[i].wait()

        def norm_step(s, carry):
            at = pl.multiple_of(WIN * i + 64 * s, 64)
            ext[pl.ds(pl.multiple_of(at + HALO, 64), 64), :] = rms_rows(xv[pl.ds(at, 64), :], gain)
            return carry

        lax.fori_loop(0, WIN // 64, norm_step, 0)
    loads[6].wait()
    wvt[...] = jnp.transpose(wq[:, 2 * features :])

    pl.semaphore_wait(barrier, len(peers))

    def remote(src, dst, send, recv, peer):
        return pltpu.make_async_remote_copy(
            src_ref=src, dst_ref=dst, send_sem=send, recv_sem=recv,
            device_id={"pix": peer}, device_id_type=MESH,
        )

    to_left = remote(fine.at[pl.ds(0, HALO)], halo.at[1], hs_sem.at[0], hr_sem.at[0], left)
    to_right = remote(
        fine.at[pl.ds(rows - HALO, HALO)], halo.at[0], hs_sem.at[1], hr_sem.at[1], right
    )
    to_left.start()
    to_right.start()

    own = [
        pltpu.make_async_copy(
            par.at[pl.ds(pl.multiple_of(16 * z, 16), 16)], zbuf.at[0, pl.ds(0, 16)], own_sem.at[0]
        ),
        pltpu.make_async_copy(pslot.at[z // 8], zslot.at[0, 0], own_sem.at[1]),
    ]
    for copy in own:
        copy.start()
    along_z = {}
    for half, ks in enumerate((NEAR, FAR)):
        for kk, k in enumerate(ks):
            if k == 0:
                continue
            there = (z + k) % ZN
            peer = there * XYN + xy
            data = remote(
                par.at[pl.ds(pl.multiple_of(16 * there, 16), 16)],
                zbuf.at[half, pl.ds(16 * kk, 16)],
                zs_sem.at[k], zr_sem.at[k], peer,
            )
            slot = remote(
                pslot.at[there // 8], zslot.at[half, kk], zss_sem.at[k], zsr_sem.at[k], peer
            )
            along_z[k] = (data, slot)
    for k in FAR + NEAR[1:]:
        along_z[k][0].start()
        along_z[k][1].start()

    lanes128 = lax.broadcasted_iota(jnp.int32, (1, 128), 1)
    lane_rows = lax.broadcasted_iota(jnp.int32, (WIN, 128), 1).astype(F32)
    head_masks = [(lanes128 // 32 == t).astype(F32).astype(BF16) for t in range(4)]

    def window(i, carry):
        w = (i + 1) % windows
        base = pl.multiple_of(w * WIN, WIN)
        own_rows = ext[pl.ds(pl.multiple_of(base + HALO, HALO), WIN), :]
        qv[pl.ds(base, WIN), :] = dot(own_rows, wq[:, :features]).astype(BF16)
        where = relb[pl.ds(base, WIN), :]
        picks = jnp.concatenate(
            [(where == lane_rows + 128.0 * c).astype(F32).astype(BF16) for c in range(4)], axis=1
        )
        gathered = dot(picks, ext[pl.ds(base, 2 * WIN), :]).astype(BF16)
        kv[...] = dot(gathered, wq[:, features : 2 * features]).astype(BF16)
        vt[...] = dot(wvt[...], gathered, NT).astype(BF16)

        def group(g, carry):
            at = pl.multiple_of(g * 128, 128)
            keys = kv[:, pl.ds(at, 128)]
            queries = qv[pl.ds(base, WIN), pl.ds(at, 128)]
            for t in range(4):
                weights = softmax_rows(dot(keys * head_masks[t], queries, NT))
                there = pl.multiple_of(at + 32 * t, 32)
                ot[pl.ds(there, 32), :] = dot(vt[pl.ds(there, 32), :], weights).astype(BF16)
            return carry

        lax.fori_loop(0, HEADS // 4, group, 0)
        acc[pl.ds(base, WIN), :] = dot(jnp.transpose(ot[...]), wo[:features, :])
        return carry

    loads[8].wait()
    lax.fori_loop(0, 2, window, 0)

    to_left.wait_recv()
    to_right.wait_recv()
    ext[:HALO, :] = rms_rows(halo[0], gain)
    ext[HALO + rows :, :] = rms_rows(halo[1], gain)
    lax.fori_loop(2, 4, window, 0)

    loads[7].wait()
    loads[9].wait()
    wpvt[...] = jnp.transpose(wp[:, features:])

    a = lax.broadcasted_iota(jnp.int32, (128, 128), 0)
    b = lax.broadcasted_iota(jnp.int32, (128, 128), 1)
    order = (b == (a % 8) * 16 + (a // 16) * 2 + (a // 8) % 2).astype(F32).astype(BF16)
    plane = []
    for half, ks in ((1, FAR), (0, NEAR)):
        for k in ks:
            for copy in own if k == 0 else along_z[k]:
                if k == 0:
                    copy.wait()
                else:
                    copy.wait_recv()
        tbuf[half] = dot(order, zbuf[half]).astype(BF16)
        for m in range(1, XYN):
            there = (xy + m) % XYN
            peer = z * XYN + there
            data = remote(
                tbuf.at[half, pl.ds(pl.multiple_of(16 * there, 16), 16)],
                fbuf.at[half, pl.ds(16 * m, 16)],
                ps_sem.at[half, m], pr_sem.at[half, m], peer,
            )
            slot = remote(
                zslot.at[half], fslot.at[half, m], pss_sem.at[half, m], psr_sem.at[half, m], peer
            )
            data.start()
            slot.start()
            plane += [data, slot]
        fbuf[half, 0:16, :] = tbuf[half, pl.ds(pl.multiple_of(16 * xy, 16), 16), :]
        fslot[half, 0] = zslot[half]

    for copy in plane:
        copy.wait_recv()
    table = fslot[...].reshape(128, 128).astype(F32).astype(BF16)
    first = 16 * (z % 8) + 2 * xy
    wanted = lax.broadcasted_iota(jnp.int32, (8, 128), 0) + first
    select = (lax.broadcasted_iota(jnp.int32, (8, 128), 1) == wanted).astype(F32).astype(BF16)
    slots = dot(select, table, NT).astype(BF16)
    ai = lax.broadcasted_iota(jnp.int32, (128, 256), 0)
    bi = lax.broadcasted_iota(jnp.int32, (128, 256), 1)
    same = (bi // 16 == ai // 8) & (bi % 8 == ai % 8)
    spread = [
        dot(slots, (same & ((bi // 8) % 2 == t)).astype(F32).astype(BF16))[t : t + 1, :]
        for t in range(2)
    ]
    position = spread[0] + spread[1]
    targets = lax.broadcasted_iota(jnp.int32, (256, 256), 0).astype(F32)
    placing = (targets == position).astype(F32).astype(BF16)
    parents = dot(placing, fbuf[...].reshape(256, features)).astype(BF16)
    pnormed = rms_rows(parents, pgv[...])
    kpv[...] = dot(pnormed, wp[:, :features]).astype(BF16)
    vpt[...] = dot(wpvt[...], pnormed, NT).astype(BF16)

    blank = jnp.zeros((PWIN, WIN), BF16)
    stores = []
    for w in range(windows):
        pair = 128 * (w // 2)

        def group(g, carry):
            at = pl.multiple_of(g * 128, 128)
            keys = kpv[PWIN * w : PWIN * (w + 1), pl.ds(at, 128)]
            queries = qv[WIN * w : WIN * (w + 1), pl.ds(at, 128)]
            for t in range(4):
                weights = softmax_rows(dot(keys * head_masks[t], queries, NT))
                parts = [weights, blank] if w % 2 == 0 else [blank, weights]
                there = pl.multiple_of(at + 32 * t, 32)
                ot[pl.ds(there, 32), :] = dot(
                    vpt[pl.ds(there, 32), pair : pair + 128], jnp.concatenate(parts, axis=0)
                ).astype(BF16)
            return carry

        lax.fori_loop(0, HEADS // 4, group, 0)
        here = slice(WIN * w, WIN * (w + 1))
        branch = acc[here, :] + dot(jnp.transpose(ot[...]), wo[features:, :])
        ov[here, :] = (xv[here, :].astype(F32) + branch).astype(BF16)
        store = pltpu.make_async_copy(
            ov.at[pl.ds(WIN * w, WIN)], out.at[pl.ds(WIN * w, WIN)], out_sem.at[w]
        )
        store.start()
        stores.append(store)

    to_left.wait_send()
    to_right.wait_send()
    for k in range(1, ZN):
        for copy in along_z[k]:
            copy.wait_send()
    for copy in plane:
        copy.wait_send()
    for store in stores:
        store.wait()


def on_device(
    fine_tokens,
    parent_tokens,
    shift_table,
    parent_slot,
    fine_gain,
    parent_gain,
    w_qkv,
    w_parent,
    w_out,
):
    rows, features = fine_tokens.shape
    dma = pltpu.SemaphoreType.DMA
    vmem = pltpu.VMEM
    return pl.pallas_call(
        kernel,
        out_shape=jax.ShapeDtypeStruct((rows, features), BF16),
        in_specs=[pl.BlockSpec(memory_space=pl.ANY)] * 9,
        out_specs=pl.BlockSpec(memory_space=pl.ANY),
        scratch_shapes=[
            vmem((rows, features), BF16),
            vmem((rows + 2 * HALO, features), BF16),
            vmem((2, HALO, features), BF16),
            vmem((rows, features), BF16),
            vmem((WIN, features), BF16),
            vmem((features, WIN), BF16),
            vmem((features, WIN), BF16),
            vmem((rows, features), F32),
            vmem((rows, 128), F32),
            vmem((8, 128), jnp.int32),
            vmem((1, features), F32),
            vmem((1, features), F32),
            vmem((features, 3 * features), BF16),
            vmem((features, 2 * features), BF16),
            vmem((2 * features, features), BF16),
            vmem((features, features), BF16),
            vmem((features, features), BF16),
            vmem((2, 128, features), BF16),
            vmem((2, 128, features), BF16),
            vmem((2, 128, features), BF16),
            vmem((2, 8, 1, 128), jnp.int32),
            vmem((2, 8, 8, 1, 128), jnp.int32),
            vmem((256, features), BF16),
            vmem((features, 256), BF16),
            vmem((rows, features), BF16),
            dma((10,)),
            dma((4,)),
            dma((2,)),
            dma((2,)),
            dma((2,)),
            dma((ZN,)),
            dma((ZN,)),
            dma((ZN,)),
            dma((ZN,)),
            dma((2, XYN)),
            dma((2, XYN)),
            dma((2, XYN)),
            dma((2, XYN)),
        ],
        compiler_params=pltpu.CompilerParams(collective_id=0, has_side_effects=True),
    )(
        fine_tokens,
        parent_tokens,
        shift_table.reshape(8, 128),
        parent_slot.reshape(2, 1, 128),
        fine_gain.reshape(1, features),
        parent_gain.reshape(1, features),
        w_qkv,
        w_parent,
        w_out,
    )


def solution(mesh):
    return jax.shard_map(
        on_device,
        mesh=mesh,
        in_specs=(
            P(("batch", "pix"), None),
            P(("batch", "pix"), None),
            P("pix"),
            P("pix"),
            P(),
            P(),
            P(),
            P(),
            P(),
        ),
        out_specs=P(("batch", "pix"), None),
        check_vma=False,
    )
```

time: 119 us -> 71 us (0.60)
  Pallas kernels: 0 us -> 68.6 us
  starting transfers between devices: 38 us -> 0 us
  local copies, waits for them, and re-layouts: 35 us -> 2.26 us
  matrix products: 28.1 us -> 0 us
  other arithmetic: 10.8 us -> 0 us
  waiting for transfers between devices: 6.59 us -> 0 us
    pallas_call x0 -> x1, Pallas kernels: none -> 68.6 us  [on_device(): pl.pallas_call(kernel, out_shape=jax.ShapeDtypeStruct((rows, features), B...]
    all_to_all x2 -> x0, starting transfers between devices: 21.6 us -> none  [the longest x1 11 us: on_device(): lax.all_to_all(parent_slot, 'pix', split_axis=0, concat_axis=0, tiled=True)]
    dot_general x6 -> x0, matrix products: 17.8 us -> none  [the longest x2 9.93 us: attend(): jnp.einsum('whrs,wshe->wrhe', weights, value_heads, preferred_element_typ...]
    ppermute x2 -> x0, starting transfers between devices: 16.4 us -> none  [the longest x1 12.9 us: with_halo(): lax.ppermute(head, axis, [((i + 1) % count, i) for i in range(count)])]
    slice x11 -> x0, local copies, waits for them, and re-layouts: 10.8 us -> none  [the longest x1 3.21 us: on_device(): extended = with_halo(qkv[:, features:], (('pix', 0),), HALO)]
    sub x1 -> x0, matrix products: 10.4 us -> none  [attend(): powers = jnp.exp(scores - highest)]
    gather x1 -> x0, local copies, waits for them, and re-layouts: 8.13 us -> none  [on_device(): window_kv = jnp.take(extended, local_index, axis=0)]
    all_to_all x2 -> x0, waiting for transfers between devices: 6.59 us -> none  [the longest x1 6.59 us: on_device(): lax.all_to_all(parent_slot, 'pix', split_axis=0, concat_axis=0, tiled=True)]
  transfers between devices with their start and end apart: 4 -> 0, of which waited for: 1 -> 0; matrix products, arithmetic and copies ran while one was open for 41% -> 0% of each run, Pallas kernels for 0% -> 0%
where the time goes in v1:
time: 71 us; the launch traced here: 70.8 us
  Pallas kernels  68.6 us (97%)
  local copies, waits for them, and re-layouts  2.26 us (3%)
    pallas_call x1, Pallas kernels, on_device(): pl.pallas_call(kernel, out_shape=jax.ShapeDtypeStruct((rows, features), B...  68.6 us
    unnamed x1, local copies, waits for them, and re-layouts  2.26 us

profile of v1, /device:TPU:4, one launch (start us, length us, event | category | flops | bytes accessed | tf_op | source)
XLA Modules:
  0.0 70.8 jit_solution(16095183076988418433)
XLA Ops:
  0.0 68.6 %shard_map.91 = bf16[1024,512]{1,0:T(8,128)(2,1)} custom-call(bf16[1024,512]{1,0:T(8,128)(2,1)} %fine.1, bf16[256,512]{1,0:T(8,128)(2,1)} %par.1, s32[8,128]{1,0:T(8,128)} %bitcast.4, s32[2,1,128]{2,1,0:T(1,128)} %bitcast.7, f32[1,512]{1,0:T(1,128)} %bitcast.5, f32[1,512]{1,0:T(1,128)} %bitcast.6, bf16[512,1536]{1,0:T(8,128)(2,1)} %wqkv.1, ...), custom_call_target="tpu_custom_call" | custom-call | tf_op jit(solution)/shard_map/pallas_call | solution.py:298
  68.6 2.3 %copy.11 = bf16[1024,512]{1,0:T(8,128)(2,1)} copy(bf16[1024,512]{1,0:T(8,128)(2,1)} %shard_map.91) | data formatting | bytes 2097152

commit v2 on v1

--- a/solution.py
+++ b/solution.py
@@ -40,13 +40,30 @@
     return (powers * (1.0 / jnp.sum(powers, axis=0, keepdims=True))).astype(BF16)
 
 
+def staged(units, depth, scores, values, sbufs, pbufs):
+    slots = len(sbufs)
+    for u in range(-2, units + 2):
+        if 0 <= u + 2 < units:
+            sbufs[(u + 2) % slots][...] = scores(u + 2)
+        if 0 <= u < units:
+            for c in range(2):
+                cols = slice(128 * c, 128 * (c + 1))
+                for first in range(0, WIN, depth):
+                    block = slice(first, first + depth)
+                    pbufs[u % slots][block, cols] = softmax_rows(sbufs[u % slots][block, cols])
+        if 0 <= u - 2 < units:
+            values(u - 2, pbufs[(u - 2) % slots][...])
+
+
 def kernel(
     fine, par, shift, pslot, fgain, pgain, wqkv, wpar, wout, out,
     xv, ext, halo, qv, kv, vt, ot, acc, relb, shv, fgv, pgv,
-    wq, wp, wo, wvt, wpvt, zbuf, tbuf, fbuf, zslot, fslot, kpv, vpt, ov,
+    wq, wp, wo, wvt, wpvt, zbuf, tbuf, fbuf, zslot, fslot, kpv, vz, cot, ov,
+    s0, s1, s2, s3, p0, p1, p2, p3,
     in_sem, out_sem, own_sem, hs_sem, hr_sem, zs_sem, zr_sem, zss_sem, zsr_sem,
     ps_sem, pr_sem, pss_sem, psr_sem,
 ):
+    sbufs, pbufs = (s0, s1, s2, s3), (p0, p1, p2, p3)
     me = lax.axis_index("pix")
     count = ZN * XYN
     z = me // XYN
@@ -164,17 +181,15 @@
         kv[...] = dot(gathered, wq[:, features : 2 * features]).astype(BF16)
         vt[...] = dot(wvt[...], gathered, NT).astype(BF16)
 
-        def group(g, carry):
-            at = pl.multiple_of(g * 128, 128)
-            keys = kv[:, pl.ds(at, 128)]
-            queries = qv[pl.ds(base, WIN), pl.ds(at, 128)]
-            for t in range(4):
-                weights = softmax_rows(dot(keys * head_masks[t], queries, NT))
-                there = pl.multiple_of(at + 32 * t, 32)
-                ot[pl.ds(there, 32), :] = dot(vt[pl.ds(there, 32), :], weights).astype(BF16)
-            return carry
-
-        lax.fori_loop(0, HEADS // 4, group, 0)
+        def self_scores(h):
+            at = 128 * (h // 4)
+            keys = kv[:, at : at + 128] * head_masks[h % 4]
+            return dot(keys, qv[pl.ds(base, WIN), at : at + 128], NT)
+
+        def self_values(h, weights):
+            ot[32 * h : 32 * h + 32, :] = dot(vt[32 * h : 32 * h + 32, :], weights).astype(BF16)
+
+        staged(HEADS, WIN, self_scores, self_values, sbufs, pbufs)
         acc[pl.ds(base, WIN), :] = dot(jnp.transpose(ot[...]), wo[:features, :])
         return carry
 
@@ -240,35 +255,38 @@
     parents = dot(placing, fbuf[...].reshape(256, features)).astype(BF16)
     pnormed = rms_rows(parents, pgv[...])
     kpv[...] = dot(pnormed, wp[:, :features]).astype(BF16)
-    vpt[...] = dot(wpvt[...], pnormed, NT).astype(BF16)
-
-    blank = jnp.zeros((PWIN, WIN), BF16)
+    block = (
+        lax.broadcasted_iota(jnp.int32, (features, WIN), 0) // 32 % 4
+        == lax.broadcasted_iota(jnp.int32, (features, WIN), 1) // PWIN
+    ).astype(F32)
+    for w in range(windows):
+        part = pnormed[PWIN * w : PWIN * (w + 1), :]
+        repeated = jnp.concatenate([part] * 4, axis=0)
+        vz[w] = (dot(wpvt[...], repeated, NT) * block).astype(BF16)
+
+    groups = HEADS // 4
     stores = []
-    for w in range(windows):
-        pair = 128 * (w // 2)
-
-        def group(g, carry):
-            at = pl.multiple_of(g * 128, 128)
-            keys = kpv[PWIN * w : PWIN * (w + 1), pl.ds(at, 128)]
-            queries = qv[WIN * w : WIN * (w + 1), pl.ds(at, 128)]
-            for t in range(4):
-                weights = softmax_rows(dot(keys * head_masks[t], queries, NT))
-                parts = [weights, blank] if w % 2 == 0 else [blank, weights]
-                there = pl.multiple_of(at + 32 * t, 32)
-                ot[pl.ds(there, 32), :] = dot(
-                    vpt[pl.ds(there, 32), pair : pair + 128], jnp.concatenate(parts, axis=0)
-                ).astype(BF16)
-            return carry
-
-        lax.fori_loop(0, HEADS // 4, group, 0)
-        here = slice(WIN * w, WIN * (w + 1))
-        branch = acc[here, :] + dot(jnp.transpose(ot[...]), wo[features:, :])
-        ov[here, :] = (xv[here, :].astype(F32) + branch).astype(BF16)
-        store = pltpu.make_async_copy(
-            ov.at[pl.ds(WIN * w, WIN)], out.at[pl.ds(WIN * w, WIN)], out_sem.at[w]
-        )
-        store.start()
-        stores.append(store)
+
+    def cross_scores(u):
+        w, at = u // groups, 128 * (u % groups)
+        keys = kpv[PWIN * w : PWIN * (w + 1), at : at + 128]
+        stacked = jnp.concatenate([keys * mask for mask in head_masks], axis=0)
+        return dot(stacked, qv[WIN * w : WIN * (w + 1), at : at + 128], NT)
+
+    def cross_values(u, weights):
+        w, at = u // groups, 128 * (u % groups)
+        cot[w, at : at + 128, :] = dot(vz[w, at : at + 128, :], weights).astype(BF16)
+        if u % groups == groups - 1:
+            here = slice(WIN * w, WIN * (w + 1))
+            branch = acc[here, :] + dot(jnp.transpose(cot[w]), wo[features:, :])
+            ov[here, :] = (xv[here, :].astype(F32) + branch).astype(BF16)
+            store = pltpu.make_async_copy(
+                ov.at[pl.ds(WIN * w, WIN)], out.at[pl.ds(WIN * w, WIN)], out_sem.at[w]
+            )
+            store.start()
+            stores.append(store)
+
+    staged(windows * groups, PWIN, cross_scores, cross_values, sbufs, pbufs)
 
     to_left.wait_send()
     to_right.wait_send()
@@ -324,8 +342,11 @@
             vmem((2, 8, 1, 128), jnp.int32),
             vmem((2, 8, 8, 1, 128), jnp.int32),
             vmem((256, features), BF16),
-            vmem((features, 256), BF16),
+            vmem((4, features, WIN), BF16),
+            vmem((4, features, WIN), BF16),
             vmem((rows, features), BF16),
+            *[vmem((WIN, WIN), F32)] * 4,
+            *[vmem((WIN, WIN), BF16)] * 4,
             dma((10,)),
             dma((4,)),
             dma((2,)),

time: 71 us -> 46.4 us (0.65)
  the two profiles are of different devices: /device:TPU:4 before, /device:TPU:30 now
where the time goes in v2:
time: 46.4 us; the launch traced here: 46.2 us
  Pallas kernels  43.9 us (95%)
  local copies, waits for them, and re-layouts  2.26 us (5%)
    pallas_call x1, Pallas kernels, on_device(): pl.pallas_call(kernel, out_shape=jax.ShapeDtypeStruct((rows, features), B...  43.9 us
    unnamed x1, local copies, waits for them, and re-layouts  2.26 us

profile of v2, /device:TPU:30, one launch (start us, length us, event | category | flops | bytes accessed | tf_op | source)
XLA Modules:
  0.0 46.2 jit_solution(739733082688645122)
XLA Ops:
  0.0 43.9 %shard_map.91 = bf16[1024,512]{1,0:T(8,128)(2,1)} custom-call(bf16[1024,512]{1,0:T(8,128)(2,1)} %fine.1, bf16[256,512]{1,0:T(8,128)(2,1)} %par.1, s32[8,128]{1,0:T(8,128)} %bitcast.4, s32[2,1,128]{2,1,0:T(1,128)} %bitcast.7, f32[1,512]{1,0:T(1,128)} %bitcast.5, f32[1,512]{1,0:T(1,128)} %bitcast.6, bf16[512,1536]{1,0:T(8,128)(2,1)} %wqkv.1, ...), custom_call_target="tpu_custom_call" | custom-call | tf_op jit(solution)/shard_map/pallas_call | solution.py:316
  44.0 2.3 %copy.11 = bf16[1024,512]{1,0:T(8,128)(2,1)} copy(bf16[1024,512]{1,0:T(8,128)(2,1)} %shard_map.91) | data formatting | bytes 2097152

commit v3 on v2

--- a/solution.py
+++ b/solution.py
@@ -61,7 +61,7 @@
     wq, wp, wo, wvt, wpvt, zbuf, tbuf, fbuf, zslot, fslot, kpv, vz, cot, ov,
     s0, s1, s2, s3, p0, p1, p2, p3,
     in_sem, out_sem, own_sem, hs_sem, hr_sem, zs_sem, zr_sem, zss_sem, zsr_sem,
-    ps_sem, pr_sem, pss_sem, psr_sem,
+    ps_sem, pr_sem, pss_sem, psr_sem, far_sem,
 ):
     sbufs, pbufs = (s0, s1, s2, s3), (p0, p1, p2, p3)
     me = lax.axis_index("pix")
@@ -87,13 +87,13 @@
     loads.append(pltpu.make_async_copy(pgain, pgv, in_sem.at[9]))
 
     barrier = pltpu.get_barrier_semaphore()
-    peers = [((z + k) % ZN) * XYN + xy for k in range(1, ZN)]
+    for load in loads:
+        load.start()
+    peers = [((z + k) % ZN) * XYN + xy for k in NEAR[1:] + (12,)]
     peers += [z * XYN + (xy + m) % XYN for m in range(1, XYN)]
     peers += [left, right]
     for peer in peers:
         pl.semaphore_signal(barrier, inc=1, device_id={"pix": peer}, device_id_type=MESH)
-    for load in loads:
-        load.start()
 
     loads[4].wait()
     loads[5].wait()
@@ -122,6 +122,9 @@
     wvt[...] = jnp.transpose(wq[:, 2 * features :])
 
     pl.semaphore_wait(barrier, len(peers))
+    for k in (4, 12):
+        peer = ((z + k) % ZN) * XYN + xy
+        pl.semaphore_signal(far_sem, inc=1, device_id={"pix": peer}, device_id_type=MESH)
 
     def remote(src, dst, send, recv, peer):
         return pltpu.make_async_remote_copy(
@@ -133,8 +136,6 @@
     to_right = remote(
         fine.at[pl.ds(rows - HALO, HALO)], halo.at[0], hs_sem.at[1], hr_sem.at[1], right
     )
-    to_left.start()
-    to_right.start()
 
     own = [
         pltpu.make_async_copy(
@@ -160,9 +161,11 @@
                 pslot.at[there // 8], zslot.at[half, kk], zss_sem.at[k], zsr_sem.at[k], peer
             )
             along_z[k] = (data, slot)
-    for k in FAR + NEAR[1:]:
+    for k in (4, 13, 3, 14, 2, 15, 1):
+        along_z[k][1].start()
         along_z[k][0].start()
-        along_z[k][1].start()
+    to_left.start()
+    to_right.start()
 
     lanes128 = lax.broadcasted_iota(jnp.int32, (1, 128), 1)
     lane_rows = lax.broadcasted_iota(jnp.int32, (WIN, 128), 1).astype(F32)
@@ -193,8 +196,55 @@
         acc[pl.ds(base, WIN), :] = dot(jnp.transpose(ot[...]), wo[:features, :])
         return carry
 
+    a = lax.broadcasted_iota(jnp.int32, (128, 128), 0)
+    b = lax.broadcasted_iota(jnp.int32, (128, 128), 1)
+    order = (b == (a % 8) * 16 + (a // 16) * 2 + (a // 8) % 2).astype(F32).astype(BF16)
+
+    def second_phase(half, ks):
+        for k in ks:
+            if k == 0:
+                own[1].wait()
+            else:
+                along_z[k][1].wait_recv()
+        slots = [
+            remote(
+                zslot.at[half], fslot.at[half, m], pss_sem.at[half, m], psr_sem.at[half, m],
+                z * XYN + (xy + m) % XYN,
+            )
+            for m in range(1, XYN)
+        ]
+        for copy in slots:
+            copy.start()
+        for k in ks:
+            if k == 0:
+                own[0].wait()
+            else:
+                along_z[k][0].wait_recv()
+        tbuf[half] = dot(order, zbuf[half]).astype(BF16)
+        fslot[half, 0] = zslot[half]
+        fbuf[half, 0:16, :] = tbuf[half, pl.ds(pl.multiple_of(16 * xy, 16), 16), :]
+        data = []
+        for m in range(1, XYN):
+            there = (xy + m) % XYN
+            data.append(
+                remote(
+                    tbuf.at[half, pl.ds(pl.multiple_of(16 * there, 16), 16)],
+                    fbuf.at[half, pl.ds(16 * m, 16)],
+                    ps_sem.at[half, m], pr_sem.at[half, m], z * XYN + there,
+                )
+            )
+        for copy in data:
+            copy.start()
+        return data, slots
+
     loads[8].wait()
-    lax.fori_loop(0, 2, window, 0)
+    lax.fori_loop(0, 1, window, 0)
+    pl.semaphore_wait(far_sem, 2)
+    for k in FAR:
+        along_z[k][1].start()
+        along_z[k][0].start()
+    lax.fori_loop(1, 2, window, 0)
+    near_data, near_slots = second_phase(0, NEAR)
 
     to_left.wait_recv()
     to_right.wait_recv()
@@ -205,37 +255,10 @@
     loads[7].wait()
     loads[9].wait()
     wpvt[...] = jnp.transpose(wp[:, features:])
-
-    a = lax.broadcasted_iota(jnp.int32, (128, 128), 0)
-    b = lax.broadcasted_iota(jnp.int32, (128, 128), 1)
-    order = (b == (a % 8) * 16 + (a // 16) * 2 + (a // 8) % 2).astype(F32).astype(BF16)
-    plane = []
-    for half, ks in ((1, FAR), (0, NEAR)):
-        for k in ks:
-            for copy in own if k == 0 else along_z[k]:
-                if k == 0:
-                    copy.wait()
-                else:
-                    copy.wait_recv()
-        tbuf[half] = dot(order, zbuf[half]).astype(BF16)
-        for m in range(1, XYN):
-            there = (xy + m) % XYN
-            peer = z * XYN + there
-            data = remote(
-                tbuf.at[half, pl.ds(pl.multiple_of(16 * there, 16), 16)],
-                fbuf.at[half, pl.ds(16 * m, 16)],
-                ps_sem.at[half, m], pr_sem.at[half, m], peer,
-            )
-            slot = remote(
-                zslot.at[half], fslot.at[half, m], pss_sem.at[half, m], psr_sem.at[half, m], peer
-            )
-            data.start()
-            slot.start()
-            plane += [data, slot]
-        fbuf[half, 0:16, :] = tbuf[half, pl.ds(pl.multiple_of(16 * xy, 16), 16), :]
-        fslot[half, 0] = zslot[half]
-
-    for copy in plane:
+    far_data, far_slots = second_phase(1, FAR)
+    plane = near_data + far_data + near_slots + far_slots
+
+    for copy in near_slots + far_slots:
         copy.wait_recv()
     table = fslot[...].reshape(128, 128).astype(F32).astype(BF16)
     first = 16 * (z % 8) + 2 * xy
@@ -252,6 +275,8 @@
     position = spread[0] + spread[1]
     targets = lax.broadcasted_iota(jnp.int32, (256, 256), 0).astype(F32)
     placing = (targets == position).astype(F32).astype(BF16)
+    for copy in near_data + far_data:
+        copy.wait_recv()
     parents = dot(placing, fbuf[...].reshape(256, features)).astype(BF16)
     pnormed = rms_rows(parents, pgv[...])
     kpv[...] = dot(pnormed, wp[:, :features]).astype(BF16)
@@ -360,6 +385,7 @@
             dma((2, XYN)),
             dma((2, XYN)),
             dma((2, XYN)),
+            pltpu.SemaphoreType.REGULAR,
         ],
         compiler_params=pltpu.CompilerParams(collective_id=0, has_side_effects=True),
     )(

time: 46.4 us -> 44.7 us (0.963)
  the two profiles are of different devices: /device:TPU:30 before, /device:TPU:4 now
where the time goes in v3:
time: 44.7 us; the launch traced here: 44.6 us
  Pallas kernels  42.3 us (95%)
  local copies, waits for them, and re-layouts  2.26 us (5%)
    pallas_call x1, Pallas kernels, on_device(): pl.pallas_call(kernel, out_shape=jax.ShapeDtypeStruct((rows, features), B...  42.3 us
    unnamed x1, local copies, waits for them, and re-layouts  2.26 us

profile of v3, /device:TPU:4, one launch (start us, length us, event | category | flops | bytes accessed | tf_op | source)
XLA Modules:
  0.0 44.6 jit_solution(6447446722527593439)
XLA Ops:
  0.0 42.3 %shard_map.91 = bf16[1024,512]{1,0:T(8,128)(2,1)} custom-call(bf16[1024,512]{1,0:T(8,128)(2,1)} %fine.1, bf16[256,512]{1,0:T(8,128)(2,1)} %par.1, s32[8,128]{1,0:T(8,128)} %bitcast.4, s32[2,1,128]{2,1,0:T(1,128)} %bitcast.7, f32[1,512]{1,0:T(1,128)} %bitcast.5, f32[1,512]{1,0:T(1,128)} %bitcast.6, bf16[512,1536]{1,0:T(8,128)(2,1)} %wqkv.1, ...), custom_call_target="tpu_custom_call" | custom-call | tf_op jit(solution)/shard_map/pallas_call | solution.py:341
  42.3 2.3 %copy.11 = bf16[1024,512]{1,0:T(8,128)(2,1)} copy(bf16[1024,512]{1,0:T(8,128)(2,1)} %shard_map.91) | data formatting | bytes 2097152

commit v4 on v3

--- a/solution.py
+++ b/solution.py
@@ -14,7 +14,7 @@
 ZN = 16
 XYN = 8
 NEAR = (0, 1, 2, 3, 4, 13, 14, 15)
-FAR = (8, 7, 9, 6, 10, 5, 11, 12)
+FAR = (5, 6, 7, 8, 9, 10, 11, 12)
 MESH = pl.DeviceIdType.MESH
 F32 = jnp.float32
 BF16 = jnp.bfloat16
@@ -58,7 +58,7 @@
 def kernel(
     fine, par, shift, pslot, fgain, pgain, wqkv, wpar, wout, out,
     xv, ext, halo, qv, kv, vt, ot, acc, relb, shv, fgv, pgv,
-    wq, wp, wo, wvt, wpvt, zbuf, tbuf, fbuf, zslot, fslot, kpv, vz, cot, ov,
+    wq, wp, wo, wvt, wpvt, zbuf, tbuf, fbuf, zslot, fslot, parv, xbuf, xslot, yslot, sslot, kpv, vz, cot, ov,
     s0, s1, s2, s3, p0, p1, p2, p3,
     in_sem, out_sem, own_sem, hs_sem, hr_sem, zs_sem, zr_sem, zss_sem, zsr_sem,
     ps_sem, pr_sem, pss_sem, psr_sem, far_sem,
@@ -85,15 +85,81 @@
     loads.append(pltpu.make_async_copy(wpar, wp, in_sem.at[7]))
     loads.append(pltpu.make_async_copy(wout, wo, in_sem.at[8]))
     loads.append(pltpu.make_async_copy(pgain, pgv, in_sem.at[9]))
+    loads.append(pltpu.make_async_copy(par, parv, in_sem.at[10]))
 
     barrier = pltpu.get_barrier_semaphore()
-    for load in loads:
-        load.start()
+    for i in (10, 0, 4, 5, 1, 2, 3, 6, 8, 7, 9):
+        loads[i].start()
     peers = [((z + k) % ZN) * XYN + xy for k in NEAR[1:] + (12,)]
     peers += [z * XYN + (xy + m) % XYN for m in range(1, XYN)]
     peers += [left, right]
     for peer in peers:
         pl.semaphore_signal(barrier, inc=1, device_id={"pix": peer}, device_id_type=MESH)
+
+    a = lax.broadcasted_iota(jnp.int32, (128, 256), 0)
+    b = lax.broadcasted_iota(jnp.int32, (128, 256), 1)
+    chosen = 16 * ((z + FAR[0] + (a // 2) % 8) % ZN) + 2 * (a // 16) + a % 2
+    pick_far = (b == chosen).astype(F32).astype(BF16)
+    loads[10].wait()
+    tbuf[1] = dot(pick_far, parv[...]).astype(BF16)
+
+    pl.semaphore_wait(barrier, len(peers))
+    for k in (4, 12):
+        peer = ((z + k) % ZN) * XYN + xy
+        pl.semaphore_signal(far_sem, inc=1, device_id={"pix": peer}, device_id_type=MESH)
+
+    def remote(src, dst, send, recv, peer):
+        return pltpu.make_async_remote_copy(
+            src_ref=src, dst_ref=dst, send_sem=send, recv_sem=recv,
+            device_id={"pix": peer}, device_id_type=MESH,
+        )
+
+    to_left = remote(fine.at[pl.ds(0, HALO)], halo.at[1], hs_sem.at[0], hr_sem.at[0], left)
+    to_right = remote(
+        fine.at[pl.ds(rows - HALO, HALO)], halo.at[0], hs_sem.at[1], hr_sem.at[1], right
+    )
+
+    own = [
+        pltpu.make_async_copy(
+            par.at[pl.ds(pl.multiple_of(16 * z, 16), 16)], zbuf.at[0, pl.ds(0, 16)], own_sem.at[0]
+        ),
+        pltpu.make_async_copy(pslot.at[z // 8], zslot.at[0], own_sem.at[1]),
+    ]
+    for copy in own:
+        copy.start()
+    own.append(pltpu.make_async_copy(pslot, xslot.at[0], own_sem.at[2]))
+    own[2].start()
+    along_z = {}
+    for kk, k in enumerate(NEAR):
+        if k == 0:
+            continue
+        there = (z + k) % ZN
+        peer = there * XYN + xy
+        data = remote(
+            par.at[pl.ds(pl.multiple_of(16 * there, 16), 16)],
+            zbuf.at[0, pl.ds(16 * kk, 16)],
+            zs_sem.at[k], zr_sem.at[k], peer,
+        )
+        slot = remote(pslot.at[there // 8], zslot.at[kk], zss_sem.at[k], zsr_sem.at[k], peer)
+        along_z[k] = (data, slot)
+    far_plane = []
+    for m in range(1, XYN):
+        there = (xy + m) % XYN
+        peer = z * XYN + there
+        data = remote(
+            tbuf.at[1, pl.ds(pl.multiple_of(16 * there, 16), 16)],
+            zbuf.at[1, pl.ds(16 * m, 16)],
+            ps_sem.at[1, m], pr_sem.at[1, m], peer,
+        )
+        slot = remote(pslot, xslot.at[m], pss_sem.at[1, m], psr_sem.at[1, m], peer)
+        far_plane.append((data, slot))
+    for i, k in enumerate((4, 12 + 1, 3, 14, 2, 15, 1)):
+        far_plane[i][1].start()
+        far_plane[i][0].start()
+        along_z[k][1].start()
+        along_z[k][0].start()
+    to_left.start()
+    to_right.start()
 
     loads[4].wait()
     loads[5].wait()
@@ -121,51 +187,42 @@
     loads[6].wait()
     wvt[...] = jnp.transpose(wq[:, 2 * features :])
 
-    pl.semaphore_wait(barrier, len(peers))
-    for k in (4, 12):
+    for data, slot in far_plane:
+        data.wait_recv()
+        slot.wait_recv()
+    own[2].wait()
+    zbuf[1, 0:16, :] = tbuf[1, pl.ds(pl.multiple_of(16 * xy, 16), 16), :]
+    a = lax.broadcasted_iota(jnp.int32, (128, 128), 0)
+    b = lax.broadcasted_iota(jnp.int32, (128, 128), 1)
+    order = (b == (a % 8) * 16 + (a // 16) * 2 + (a // 8) % 2).astype(F32).astype(BF16)
+    xbuf[...] = dot(order, zbuf[1]).astype(BF16)
+    tables = xslot[...].reshape(16, 128).astype(F32)
+    tables = tables.reshape(8, 2, 128)
+    tables = jnp.concatenate([tables[:, 0, :], tables[:, 1, :]], axis=1)
+    ka = lax.broadcasted_iota(jnp.int32, (8, 256), 0)
+    kb = lax.broadcasted_iota(jnp.int32, (8, 256), 1)
+    slots = None
+    for t in range(2):
+        hit = (kb == 16 * ((z + FAR[0] + ka) % ZN) + 2 * xy + t).astype(F32).astype(BF16)
+        parts = [jnp.zeros((8, 256), F32)] * 16
+        parts[t] = tables
+        part = dot(hit, jnp.concatenate(parts, axis=0).astype(BF16), NT)
+        slots = part if slots is None else slots + part
+    for kk in range(8):
+        yslot[kk] = slots[kk : kk + 1, :]
+    far_z = []
+    for kk, k in enumerate(FAR):
         peer = ((z + k) % ZN) * XYN + xy
-        pl.semaphore_signal(far_sem, inc=1, device_id={"pix": peer}, device_id_type=MESH)
-
-    def remote(src, dst, send, recv, peer):
-        return pltpu.make_async_remote_copy(
-            src_ref=src, dst_ref=dst, send_sem=send, recv_sem=recv,
-            device_id={"pix": peer}, device_id_type=MESH,
-        )
-
-    to_left = remote(fine.at[pl.ds(0, HALO)], halo.at[1], hs_sem.at[0], hr_sem.at[0], left)
-    to_right = remote(
-        fine.at[pl.ds(rows - HALO, HALO)], halo.at[0], hs_sem.at[1], hr_sem.at[1], right
-    )
-
-    own = [
-        pltpu.make_async_copy(
-            par.at[pl.ds(pl.multiple_of(16 * z, 16), 16)], zbuf.at[0, pl.ds(0, 16)], own_sem.at[0]
-        ),
-        pltpu.make_async_copy(pslot.at[z // 8], zslot.at[0, 0], own_sem.at[1]),
-    ]
-    for copy in own:
-        copy.start()
-    along_z = {}
-    for half, ks in enumerate((NEAR, FAR)):
-        for kk, k in enumerate(ks):
-            if k == 0:
-                continue
-            there = (z + k) % ZN
-            peer = there * XYN + xy
-            data = remote(
-                par.at[pl.ds(pl.multiple_of(16 * there, 16), 16)],
-                zbuf.at[half, pl.ds(16 * kk, 16)],
-                zs_sem.at[k], zr_sem.at[k], peer,
-            )
-            slot = remote(
-                pslot.at[there // 8], zslot.at[half, kk], zss_sem.at[k], zsr_sem.at[k], peer
-            )
-            along_z[k] = (data, slot)
-    for k in (4, 13, 3, 14, 2, 15, 1):
-        along_z[k][1].start()
-        along_z[k][0].start()
-    to_left.start()
-    to_right.start()
+        data = remote(
+            xbuf.at[pl.ds(16 * kk, 16)], fbuf.at[1, pl.ds(16 * kk, 16)],
+            zs_sem.at[k], zr_sem.at[k], peer,
+        )
+        slot = remote(yslot.at[kk], sslot.at[kk], zss_sem.at[k], zsr_sem.at[k], peer)
+        far_z.append((data, slot))
+    pl.semaphore_wait(far_sem, 2)
+    for i in (3, 4, 2, 5, 1, 6, 0, 7):
+        far_z[i][1].start()
+        far_z[i][0].start()
 
     lanes128 = lax.broadcasted_iota(jnp.int32, (1, 128), 1)
     lane_rows = lax.broadcasted_iota(jnp.int32, (WIN, 128), 1).astype(F32)
@@ -196,41 +253,37 @@
         acc[pl.ds(base, WIN), :] = dot(jnp.transpose(ot[...]), wo[:features, :])
         return carry
 
-    a = lax.broadcasted_iota(jnp.int32, (128, 128), 0)
-    b = lax.broadcasted_iota(jnp.int32, (128, 128), 1)
-    order = (b == (a % 8) * 16 + (a // 16) * 2 + (a // 8) % 2).astype(F32).astype(BF16)
-
-    def second_phase(half, ks):
-        for k in ks:
+    def near_phase():
+        for k in NEAR:
             if k == 0:
                 own[1].wait()
             else:
                 along_z[k][1].wait_recv()
         slots = [
             remote(
-                zslot.at[half], fslot.at[half, m], pss_sem.at[half, m], psr_sem.at[half, m],
+                zslot, fslot.at[m], pss_sem.at[0, m], psr_sem.at[0, m],
                 z * XYN + (xy + m) % XYN,
             )
             for m in range(1, XYN)
         ]
         for copy in slots:
             copy.start()
-        for k in ks:
+        for k in NEAR:
             if k == 0:
                 own[0].wait()
             else:
                 along_z[k][0].wait_recv()
-        tbuf[half] = dot(order, zbuf[half]).astype(BF16)
-        fslot[half, 0] = zslot[half]
-        fbuf[half, 0:16, :] = tbuf[half, pl.ds(pl.multiple_of(16 * xy, 16), 16), :]
+        tbuf[0] = dot(order, zbuf[0]).astype(BF16)
+        fslot[0] = zslot[...]
+        fbuf[0, 0:16, :] = tbuf[0, pl.ds(pl.multiple_of(16 * xy, 16), 16), :]
         data = []
         for m in range(1, XYN):
             there = (xy + m) % XYN
             data.append(
                 remote(
-                    tbuf.at[half, pl.ds(pl.multiple_of(16 * there, 16), 16)],
-                    fbuf.at[half, pl.ds(16 * m, 16)],
-                    ps_sem.at[half, m], pr_sem.at[half, m], z * XYN + there,
+                    tbuf.at[0, pl.ds(pl.multiple_of(16 * there, 16), 16)],
+                    fbuf.at[0, pl.ds(16 * m, 16)],
+                    ps_sem.at[0, m], pr_sem.at[0, m], z * XYN + there,
                 )
             )
         for copy in data:
@@ -239,12 +292,8 @@
 
     loads[8].wait()
     lax.fori_loop(0, 1, window, 0)
-    pl.semaphore_wait(far_sem, 2)
-    for k in FAR:
-        along_z[k][1].start()
-        along_z[k][0].start()
+    near_data, near_slots = near_phase()
     lax.fori_loop(1, 2, window, 0)
-    near_data, near_slots = second_phase(0, NEAR)
 
     to_left.wait_recv()
     to_right.wait_recv()
@@ -255,27 +304,33 @@
     loads[7].wait()
     loads[9].wait()
     wpvt[...] = jnp.transpose(wp[:, features:])
-    far_data, far_slots = second_phase(1, FAR)
-    plane = near_data + far_data + near_slots + far_slots
-
-    for copy in near_slots + far_slots:
+
+    for copy in near_slots:
         copy.wait_recv()
-    table = fslot[...].reshape(128, 128).astype(F32).astype(BF16)
+    table = jnp.concatenate([fslot[...].reshape(64, 128).astype(F32), jnp.zeros((64, 128), F32)], axis=0)
     first = 16 * (z % 8) + 2 * xy
     wanted = lax.broadcasted_iota(jnp.int32, (8, 128), 0) + first
     select = (lax.broadcasted_iota(jnp.int32, (8, 128), 1) == wanted).astype(F32).astype(BF16)
-    slots = dot(select, table, NT).astype(BF16)
-    ai = lax.broadcasted_iota(jnp.int32, (128, 256), 0)
-    bi = lax.broadcasted_iota(jnp.int32, (128, 256), 1)
-    same = (bi // 16 == ai // 8) & (bi % 8 == ai % 8)
+    slots = dot(select, table.astype(BF16), NT).astype(BF16)
+    same = (b // 16 == a // 8) & (b % 8 == a % 8)
     spread = [
-        dot(slots, (same & ((bi // 8) % 2 == t)).astype(F32).astype(BF16))[t : t + 1, :]
+        dot(slots, (same & ((b // 8) % 2 == t)).astype(F32).astype(BF16))[t : t + 1, :]
         for t in range(2)
     ]
-    position = spread[0] + spread[1]
+    near_position = spread[0] + spread[1]
+    for data, slot in far_z:
+        slot.wait_recv()
+    slots = dot(
+        sslot[...].reshape(8, 128).astype(BF16), (a == b % 16).astype(F32).astype(BF16)
+    )
+    held = lax.broadcasted_iota(jnp.int32, (8, 128), 1) // 16 == lax.broadcasted_iota(
+        jnp.int32, (8, 128), 0
+    )
+    far_position = jnp.sum(jnp.where(held, slots, 0.0), axis=0, keepdims=True)
+    position = jnp.concatenate([near_position, far_position], axis=1)
     targets = lax.broadcasted_iota(jnp.int32, (256, 256), 0).astype(F32)
     placing = (targets == position).astype(F32).astype(BF16)
-    for copy in near_data + far_data:
+    for copy in near_data + [data for data, slot in far_z]:
         copy.wait_recv()
     parents = dot(placing, fbuf[...].reshape(256, features)).astype(BF16)
     pnormed = rms_rows(parents, pgv[...])
@@ -315,10 +370,10 @@
 
     to_left.wait_send()
     to_right.wait_send()
-    for k in range(1, ZN):
-        for copy in along_z[k]:
+    for pair in list(along_z.values()) + far_plane + far_z:
+        for copy in pair:
             copy.wait_send()
-    for copy in plane:
+    for copy in near_data + near_slots:
         copy.wait_send()
     for store in stores:
         store.wait()
@@ -364,17 +419,22 @@
             vmem((2, 128, features), BF16),
             vmem((2, 128, features), BF16),
             vmem((2, 128, features), BF16),
-            vmem((2, 8, 1, 128), jnp.int32),
-            vmem((2, 8, 8, 1, 128), jnp.int32),
+            vmem((8, 1, 128), jnp.int32),
+            vmem((8, 8, 1, 128), jnp.int32),
+            vmem((256, features), BF16),
+            vmem((128, features), BF16),
+            vmem((8, 2, 1, 128), jnp.int32),
+            vmem((8, 1, 128), F32),
+            vmem((8, 1, 128), F32),
             vmem((256, features), BF16),
             vmem((4, features, WIN), BF16),
             vmem((4, features, WIN), BF16),
             vmem((rows, features), BF16),
             *[vmem((WIN, WIN), F32)] * 4,
             *[vmem((WIN, WIN), BF16)] * 4,
-            dma((10,)),
+            dma((11,)),
             dma((4,)),
-            dma((2,)),
+            dma((3,)),
             dma((2,)),
             dma((2,)),
             dma((ZN,)),

time: 44.7 us -> 40.9 us (0.915)
  Pallas kernels: 42.3 us -> 38.5 us
    pallas_call x1, Pallas kernels: 42.3 us -> 38.5 us  [on_device(): pl.pallas_call(kernel, out_shape=jax.ShapeDtypeStruct((rows, features), B...]
where the time goes in v4:
time: 40.9 us; the launch traced here: 40.8 us
  Pallas kernels  38.5 us (94%)
  local copies, waits for them, and re-layouts  2.26 us (6%)
    pallas_call x1, Pallas kernels, on_device(): pl.pallas_call(kernel, out_shape=jax.ShapeDtypeStruct((rows, features), B...  38.5 us
    unnamed x1, local copies, waits for them, and re-layouts  2.26 us

profile of v4, /device:TPU:4, one launch (start us, length us, event | category | flops | bytes accessed | tf_op | source)
XLA Modules:
  0.0 40.8 jit_solution(15201002868895374041)
XLA Ops:
  0.0 38.5 %shard_map.91 = bf16[1024,512]{1,0:T(8,128)(2,1)} custom-call(bf16[1024,512]{1,0:T(8,128)(2,1)} %fine.1, bf16[256,512]{1,0:T(8,128)(2,1)} %par.1, s32[8,128]{1,0:T(8,128)} %bitcast.4, s32[2,1,128]{2,1,0:T(1,128)} %bitcast.7, f32[1,512]{1,0:T(1,128)} %bitcast.5, f32[1,512]{1,0:T(1,128)} %bitcast.6, bf16[512,1536]{1,0:T(8,128)(2,1)} %wqkv.1, ...), custom_call_target="tpu_custom_call" | custom-call | tf_op jit(solution)/shard_map/pallas_call | solution.py:396
  38.5 2.3 %copy.11 = bf16[1024,512]{1,0:T(8,128)(2,1)} copy(bf16[1024,512]{1,0:T(8,128)(2,1)} %shard_map.91) | data formatting | bytes 2097152

commit v5 on v4

--- a/solution.py
+++ b/solution.py
@@ -56,9 +56,9 @@
 
 
 def kernel(
-    fine, par, shift, pslot, fgain, pgain, wqkv, wpar, wout, out,
-    xv, ext, halo, qv, kv, vt, ot, acc, relb, shv, fgv, pgv,
-    wq, wp, wo, wvt, wpvt, zbuf, tbuf, fbuf, zslot, fslot, parv, xbuf, xslot, yslot, sslot, kpv, vz, cot, ov,
+    fine, par, shift, pslot, fgain, pgain, wqkv, wpar, out,
+    xv, ext, halo, qv, kv, vt, ot, relb, shv, fgv, pgv,
+    wq, wp, wvt, zbuf, tbuf, fbuf, zslot, fslot, parv, xbuf, xslot, yslot, sslot, kpv, cot, ov,
     s0, s1, s2, s3, p0, p1, p2, p3,
     in_sem, out_sem, own_sem, hs_sem, hr_sem, zs_sem, zr_sem, zss_sem, zsr_sem,
     ps_sem, pr_sem, pss_sem, psr_sem, far_sem,
@@ -83,12 +83,11 @@
     loads.append(pltpu.make_async_copy(shift, shv, in_sem.at[5]))
     loads.append(pltpu.make_async_copy(wqkv, wq, in_sem.at[6]))
     loads.append(pltpu.make_async_copy(wpar, wp, in_sem.at[7]))
-    loads.append(pltpu.make_async_copy(wout, wo, in_sem.at[8]))
-    loads.append(pltpu.make_async_copy(pgain, pgv, in_sem.at[9]))
-    loads.append(pltpu.make_async_copy(par, parv, in_sem.at[10]))
+    loads.append(pltpu.make_async_copy(pgain, pgv, in_sem.at[8]))
+    loads.append(pltpu.make_async_copy(par, parv, in_sem.at[9]))
 
     barrier = pltpu.get_barrier_semaphore()
-    for i in (10, 0, 4, 5, 1, 2, 3, 6, 8, 7, 9):
+    for i in (9, 0, 4, 5, 1, 2, 3, 6, 7, 8):
         loads[i].start()
     peers = [((z + k) % ZN) * XYN + xy for k in NEAR[1:] + (12,)]
     peers += [z * XYN + (xy + m) % XYN for m in range(1, XYN)]
@@ -100,7 +99,7 @@
     b = lax.broadcasted_iota(jnp.int32, (128, 256), 1)
     chosen = 16 * ((z + FAR[0] + (a // 2) % 8) % ZN) + 2 * (a // 16) + a % 2
     pick_far = (b == chosen).astype(F32).astype(BF16)
-    loads[10].wait()
+    loads[9].wait()
     tbuf[1] = dot(pick_far, parv[...]).astype(BF16)
 
     pl.semaphore_wait(barrier, len(peers))
@@ -250,7 +249,7 @@
             ot[32 * h : 32 * h + 32, :] = dot(vt[32 * h : 32 * h + 32, :], weights).astype(BF16)
 
         staged(HEADS, WIN, self_scores, self_values, sbufs, pbufs)
-        acc[pl.ds(base, WIN), :] = dot(jnp.transpose(ot[...]), wo[:features, :])
+        ov[pl.ds(base, WIN), :features] = jnp.transpose(ot[...])
         return carry
 
     def near_phase():
@@ -290,7 +289,6 @@
             copy.start()
         return data, slots
 
-    loads[8].wait()
     lax.fori_loop(0, 1, window, 0)
     near_data, near_slots = near_phase()
     lax.fori_loop(1, 2, window, 0)
@@ -301,9 +299,13 @@
     ext[HALO + rows :, :] = rms_rows(halo[1], gain)
     lax.fori_loop(2, 4, window, 0)
 
+    self_store = pltpu.make_async_copy(
+        ov.at[:, pl.ds(0, features)], out.at[:, pl.ds(0, features)], out_sem.at[4]
+    )
+    self_store.start()
+    stores = [self_store]
     loads[7].wait()
-    loads[9].wait()
-    wpvt[...] = jnp.transpose(wp[:, features:])
+    loads[8].wait()
 
     for copy in near_slots:
         copy.wait_recv()
@@ -334,18 +336,8 @@
         copy.wait_recv()
     parents = dot(placing, fbuf[...].reshape(256, features)).astype(BF16)
     pnormed = rms_rows(parents, pgv[...])
-    kpv[...] = dot(pnormed, wp[:, :features]).astype(BF16)
-    block = (
-        lax.broadcasted_iota(jnp.int32, (features, WIN), 0) // 32 % 4
-        == lax.broadcasted_iota(jnp.int32, (features, WIN), 1) // PWIN
-    ).astype(F32)
-    for w in range(windows):
-        part = pnormed[PWIN * w : PWIN * (w + 1), :]
-        repeated = jnp.concatenate([part] * 4, axis=0)
-        vz[w] = (dot(wpvt[...], repeated, NT) * block).astype(BF16)
-
+    kpv[...] = dot(pnormed, wp[...]).astype(BF16)
     groups = HEADS // 4
-    stores = []
 
     def cross_scores(u):
         w, at = u // groups, 128 * (u % groups)
@@ -355,13 +347,16 @@
 
     def cross_values(u, weights):
         w, at = u // groups, 128 * (u % groups)
-        cot[w, at : at + 128, :] = dot(vz[w, at : at + 128, :], weights).astype(BF16)
+        part = kpv[PWIN * w : PWIN * (w + 1), features + at : features + at + 128]
+        stacked = jnp.concatenate([part * mask for mask in head_masks], axis=0)
+        cot[w, at : at + 128, :] = dot(stacked, weights, TN).astype(BF16)
         if u % groups == groups - 1:
             here = slice(WIN * w, WIN * (w + 1))
-            branch = acc[here, :] + dot(jnp.transpose(cot[w]), wo[features:, :])
-            ov[here, :] = (xv[here, :].astype(F32) + branch).astype(BF16)
+            ov[here, features:] = jnp.transpose(cot[w])
             store = pltpu.make_async_copy(
-                ov.at[pl.ds(WIN * w, WIN)], out.at[pl.ds(WIN * w, WIN)], out_sem.at[w]
+                ov.at[pl.ds(WIN * w, WIN), pl.ds(features, features)],
+                out.at[pl.ds(WIN * w, WIN), pl.ds(features, features)],
+                out_sem.at[w],
             )
             store.start()
             stores.append(store)
@@ -393,10 +388,10 @@
     rows, features = fine_tokens.shape
     dma = pltpu.SemaphoreType.DMA
     vmem = pltpu.VMEM
-    return pl.pallas_call(
+    joined = pl.pallas_call(
         kernel,
-        out_shape=jax.ShapeDtypeStruct((rows, features), BF16),
-        in_specs=[pl.BlockSpec(memory_space=pl.ANY)] * 9,
+        out_shape=jax.ShapeDtypeStruct((rows, 2 * features), BF16),
+        in_specs=[pl.BlockSpec(memory_space=pl.ANY)] * 8,
         out_specs=pl.BlockSpec(memory_space=pl.ANY),
         scratch_shapes=[
             vmem((rows, features), BF16),
@@ -406,15 +401,12 @@
             vmem((WIN, features), BF16),
             vmem((features, WIN), BF16),
             vmem((features, WIN), BF16),
-            vmem((rows, features), F32),
             vmem((rows, 128), F32),
             vmem((8, 128), jnp.int32),
             vmem((1, features), F32),
             vmem((1, features), F32),
             vmem((features, 3 * features), BF16),
             vmem((features, 2 * features), BF16),
-            vmem((2 * features, features), BF16),
-            vmem((features, features), BF16),
             vmem((features, features), BF16),
             vmem((2, 128, features), BF16),
             vmem((2, 128, features), BF16),
@@ -426,14 +418,13 @@
             vmem((8, 2, 1, 128), jnp.int32),
             vmem((8, 1, 128), F32),
             vmem((8, 1, 128), F32),
-            vmem((256, features), BF16),
+            vmem((256, 2 * features), BF16),
             vmem((4, features, WIN), BF16),
-            vmem((4, features, WIN), BF16),
-            vmem((rows, features), BF16),
+            vmem((rows, 2 * features), BF16),
             *[vmem((WIN, WIN), F32)] * 4,
             *[vmem((WIN, WIN), BF16)] * 4,
-            dma((11,)),
-            dma((4,)),
+            dma((10,)),
+            dma((5,)),
             dma((3,)),
             dma((2,)),
             dma((2,)),
@@ -447,18 +438,24 @@
             dma((2, XYN)),
             pltpu.SemaphoreType.REGULAR,
         ],
-        compiler_params=pltpu.CompilerParams(collective_id=0, has_side_effects=True),
+        compiler_params=pltpu.CompilerParams(collective_id=0, has_side_effects=True, vmem_limit_bytes=25165824),
     )(
-        fine_tokens,
-        parent_tokens,
-        shift_table.reshape(8, 128),
-        parent_slot.reshape(2, 1, 128),
-        fine_gain.reshape(1, features),
-        parent_gain.reshape(1, features),
-        w_qkv,
-        w_parent,
-        w_out,
-    )
+        *[
+            pltpu.with_memory_space_constraint(x, pltpu.HBM)
+            for x in (
+                fine_tokens,
+                parent_tokens,
+                shift_table.reshape(8, 128),
+                parent_slot.reshape(2, 1, 128),
+                fine_gain.reshape(1, features),
+                parent_gain.reshape(1, features),
+                w_qkv,
+                w_parent,
+            )
+        ]
+    )
+    branch = jnp.dot(joined, w_out, preferred_element_type=F32)
+    return (fine_tokens.astype(F32) + branch).astype(BF16)
 
 
 def solution(mesh):

time: 40.9 us -> 39.5 us (0.966)
  local copies, waits for them, and re-layouts: 2.26 us -> 0.01 us
  matrix products: 0 us -> 2.22 us
  Pallas kernels: 38.5 us -> 37.1 us
    unnamed x1 -> x4, local copies, waits for them, and re-layouts: 2.26 us -> 0.01 us
    dot_general x0 -> x1, matrix products: none -> 2.22 us  [on_device(): branch = jnp.dot(joined, w_out, preferred_element_type=F32)]
    pallas_call x1, Pallas kernels: 38.5 us -> 37.1 us  [on_device(): pl.pallas_call(kernel, out_shape=jax.ShapeDtypeStruct((rows, 2 * features...]
where the time goes in v5:
time: 39.5 us; the launch traced here: 39.4 us
  Pallas kernels  37.1 us (94%)
  matrix products  2.22 us (6%)
    pallas_call x1, Pallas kernels, on_device(): pl.pallas_call(kernel, out_shape=jax.ShapeDtypeStruct((rows, 2 * features...  37.1 us
    dot_general x1, matrix products, on_device(): branch = jnp.dot(joined, w_out, preferred_element_type=F32)  2.22 us

profile of v5, /device:TPU:4, one launch (start us, length us, event | category | flops | bytes accessed | tf_op | source)
XLA Modules:
  0.0 39.4 jit_solution(905257339803577805)
XLA Ops:
  0.0 0.0 copy-start
  0.0 0.0 copy-start.1
  0.0 37.1 %shard_map.91 = bf16[1024,1024]{1,0:T(8,128)(2,1)S(1)} custom-call(bf16[1024,512]{1,0:T(8,128)(2,1)} %fine.1, bf16[256,512]{1,0:T(8,128)(2,1)} %par.1, s32[8,128]{1,0:T(8,128)} %bitcast.6, s32[2,1,128]{2,1,0:T(1,128)} %bitcast.9, f32[1,512]{1,0:T(1,128)} %bitcast.7, f32[1,512]{1,0:T(1,128)} %bitcast.8, bf16[512,1536]{1,0:T(8,128)(2,1)} %wqkv.1, ...), custom_call_target="tpu_custom_call" | custom-call | tf_op jit(solution)/shard_map/pallas_call | solution.py:391
  37.2 0.0 copy-done
  37.2 0.0 copy-done.1
  37.2 2.2 %add_convert_fusion = bf16[1024,512]{1,0:T(8,128)(2,1)} fusion(bf16[1024,512]{1,0:T(8,128)(2,1)S(1)} %copy-done.1, bf16[1024,1024]{1,0:T(8,128)(2,1)S(1)} %shard_map.91, bf16[1024,512]{1,0:T(8,128)(2,1)S(1)} %copy-done), kind=kOutput, calls=%fused_computation | convolution fusion | flops 1075314688 | bytes 5242880 | tf_op jit(solution)/shard_map/dot_general | solution.py:457
Async XLA Ops:
  0.0 37.2 %copy-start = (bf16[1024,512]{1,0:T(8,128)(2,1)S(1)}, bf16[1024,512]{1,0:T(8,128)(2,1)}, u32[]{:S(2)}) copy-start(bf16[1024,512]{1,0:T(8,128)(2,1)} %param.17) | copy-start | bytes 3145732
  0.0 37.2 %copy-start.1 = (bf16[1024,512]{1,0:T(8,128)(2,1)S(1)}, bf16[1024,512]{1,0:T(8,128)(2,1)}, u32[]{:S(2)}) copy-start(bf16[1024,512]{1,0:T(8,128)(2,1)} %fine.1) | copy-start | bytes 3145732

commit v6 on v5

--- a/solution.py
+++ b/solution.py
@@ -58,9 +58,9 @@
 def kernel(
     fine, par, shift, pslot, fgain, pgain, wqkv, wpar, out,
     xv, ext, halo, qv, kv, vt, ot, relb, shv, fgv, pgv,
-    wq, wp, wvt, zbuf, tbuf, fbuf, zslot, fslot, parv, xbuf, xslot, yslot, sslot, kpv, cot, ov,
+    wq, wp, wvt, zbuf, tbuf, fbuf, zslot, fslot, parv, xbuf, xslot, yslot, sslot, kpv, cot,
     s0, s1, s2, s3, p0, p1, p2, p3,
-    in_sem, out_sem, own_sem, hs_sem, hr_sem, zs_sem, zr_sem, zss_sem, zsr_sem,
+    in_sem, own_sem, hs_sem, hr_sem, zs_sem, zr_sem, zss_sem, zsr_sem,
     ps_sem, pr_sem, pss_sem, psr_sem, far_sem,
 ):
     sbufs, pbufs = (s0, s1, s2, s3), (p0, p1, p2, p3)
@@ -157,9 +157,6 @@
         far_plane[i][0].start()
         along_z[k][1].start()
         along_z[k][0].start()
-    to_left.start()
-    to_right.start()
-
     loads[4].wait()
     loads[5].wait()
     place = lax.broadcasted_iota(jnp.int32, (8, 128), 0) * 128 + lax.broadcasted_iota(
@@ -187,14 +184,8 @@
     wvt[...] = jnp.transpose(wq[:, 2 * features :])
 
     for data, slot in far_plane:
-        data.wait_recv()
         slot.wait_recv()
     own[2].wait()
-    zbuf[1, 0:16, :] = tbuf[1, pl.ds(pl.multiple_of(16 * xy, 16), 16), :]
-    a = lax.broadcasted_iota(jnp.int32, (128, 128), 0)
-    b = lax.broadcasted_iota(jnp.int32, (128, 128), 1)
-    order = (b == (a % 8) * 16 + (a // 16) * 2 + (a // 8) % 2).astype(F32).astype(BF16)
-    xbuf[...] = dot(order, zbuf[1]).astype(BF16)
     tables = xslot[...].reshape(16, 128).astype(F32)
     tables = tables.reshape(8, 2, 128)
     tables = jnp.concatenate([tables[:, 0, :], tables[:, 1, :]], axis=1)
@@ -209,6 +200,13 @@
         slots = part if slots is None else slots + part
     for kk in range(8):
         yslot[kk] = slots[kk : kk + 1, :]
+    for data, slot in far_plane:
+        data.wait_recv()
+    zbuf[1, 0:16, :] = tbuf[1, pl.ds(pl.multiple_of(16 * xy, 16), 16), :]
+    a = lax.broadcasted_iota(jnp.int32, (128, 128), 0)
+    b = lax.broadcasted_iota(jnp.int32, (128, 128), 1)
+    order = (b == (a % 8) * 16 + (a // 16) * 2 + (a // 8) % 2).astype(F32).astype(BF16)
+    xbuf[...] = dot(order, zbuf[1]).astype(BF16)
     far_z = []
     for kk, k in enumerate(FAR):
         peer = ((z + k) % ZN) * XYN + xy
@@ -221,7 +219,10 @@
     pl.semaphore_wait(far_sem, 2)
     for i in (3, 4, 2, 5, 1, 6, 0, 7):
         far_z[i][1].start()
+    for i in (3, 4, 2, 5, 1, 6, 0, 7):
         far_z[i][0].start()
+    to_left.start()
+    to_right.start()
 
     lanes128 = lax.broadcasted_iota(jnp.int32, (1, 128), 1)
     lane_rows = lax.broadcasted_iota(jnp.int32, (WIN, 128), 1).astype(F32)
@@ -249,7 +250,7 @@
             ot[32 * h : 32 * h + 32, :] = dot(vt[32 * h : 32 * h + 32, :], weights).astype(BF16)
 
         staged(HEADS, WIN, self_scores, self_values, sbufs, pbufs)
-        ov[pl.ds(base, WIN), :features] = jnp.transpose(ot[...])
+        out[pl.ds(base, WIN), :features] = jnp.transpose(ot[...])
         return carry
 
     def near_phase():
@@ -299,11 +300,6 @@
     ext[HALO + rows :, :] = rms_rows(halo[1], gain)
     lax.fori_loop(2, 4, window, 0)
 
-    self_store = pltpu.make_async_copy(
-        ov.at[:, pl.ds(0, features)], out.at[:, pl.ds(0, features)], out_sem.at[4]
-    )
-    self_store.start()
-    stores = [self_store]
     loads[7].wait()
     loads[8].wait()
 
@@ -332,6 +328,13 @@
     position = jnp.concatenate([near_position, far_position], axis=1)
     targets = lax.broadcasted_iota(jnp.int32, (256, 256), 0).astype(F32)
     placing = (targets == position).astype(F32).astype(BF16)
+    to_left.wait_send()
+    to_right.wait_send()
+    for pair in list(along_z.values()) + far_plane + far_z:
+        for copy in pair:
+            copy.wait_send()
+    for copy in near_data + near_slots:
+        copy.wait_send()
     for copy in near_data + [data for data, slot in far_z]:
         copy.wait_recv()
     parents = dot(placing, fbuf[...].reshape(256, features)).astype(BF16)
@@ -352,26 +355,9 @@
         cot[w, at : at + 128, :] = dot(stacked, weights, TN).astype(BF16)
         if u % groups == groups - 1:
             here = slice(WIN * w, WIN * (w + 1))
-            ov[here, features:] = jnp.transpose(cot[w])
-            store = pltpu.make_async_copy(
-                ov.at[pl.ds(WIN * w, WIN), pl.ds(features, features)],
-                out.at[pl.ds(WIN * w, WIN), pl.ds(features, features)],
-                out_sem.at[w],
-            )
-            store.start()
-            stores.append(store)
+            out[here, features:] = jnp.transpose(cot[w])
 
     staged(windows * groups, PWIN, cross_scores, cross_values, sbufs, pbufs)
-
-    to_left.wait_send()
-    to_right.wait_send()
-    for pair in list(along_z.values()) + far_plane + far_z:
-        for copy in pair:
-            copy.wait_send()
-    for copy in near_data + near_slots:
-        copy.wait_send()
-    for store in stores:
-        store.wait()
 
 
 def on_device(
@@ -392,7 +378,7 @@
         kernel,
         out_shape=jax.ShapeDtypeStruct((rows, 2 * features), BF16),
         in_specs=[pl.BlockSpec(memory_space=pl.ANY)] * 8,
-        out_specs=pl.BlockSpec(memory_space=pl.ANY),
+        out_specs=pl.BlockSpec(memory_space=pltpu.VMEM),
         scratch_shapes=[
             vmem((rows, features), BF16),
             vmem((rows + 2 * HALO, features), BF16),
@@ -420,11 +406,9 @@
             vmem((8, 1, 128), F32),
             vmem((256, 2 * features), BF16),
             vmem((4, features, WIN), BF16),
-            vmem((rows, 2 * features), BF16),
             *[vmem((WIN, WIN), F32)] * 4,
             *[vmem((WIN, WIN), BF16)] * 4,
             dma((10,)),
-            dma((5,)),
             dma((3,)),
             dma((2,)),
             dma((2,)),

time: 39.5 us -> 45 us (1.14)
  the two profiles are of different devices: /device:TPU:4 before, /device:TPU:1 now
where the time goes in v6:
time: 45 us; the launch traced here: 44.9 us
  Pallas kernels  42.6 us (95%)
  matrix products  2.22 us (5%)
    pallas_call x1, Pallas kernels, on_device(): pl.pallas_call(kernel, out_shape=jax.ShapeDtypeStruct((rows, 2 * features...  42.6 us
    dot_general x1, matrix products, on_device(): branch = jnp.dot(joined, w_out, preferred_element_type=F32)  2.22 us

profile of v6, /device:TPU:1, one launch (start us, length us, event | category | flops | bytes accessed | tf_op | source)
XLA Modules:
  0.0 44.9 jit_solution(2030306108101853236)
XLA Ops:
  0.0 0.0 copy-start
  0.0 0.0 copy-start.1
  0.0 42.6 %shard_map.91 = bf16[1024,1024]{1,0:T(8,128)(2,1)S(1)} custom-call(bf16[1024,512]{1,0:T(8,128)(2,1)} %fine.1, bf16[256,512]{1,0:T(8,128)(2,1)} %par.1, s32[8,128]{1,0:T(8,128)} %bitcast.6, s32[2,1,128]{2,1,0:T(1,128)} %bitcast.9, f32[1,512]{1,0:T(1,128)} %bitcast.7, f32[1,512]{1,0:T(1,128)} %bitcast.8, bf16[512,1536]{1,0:T(8,128)(2,1)} %wqkv.1, ...), custom_call_target="tpu_custom_call" | custom-call | tf_op jit(solution)/shard_map/pallas_call | solution.py:377
  42.7 0.0 copy-done
  42.7 0.0 copy-done.1
  42.7 2.2 %add_convert_fusion = bf16[1024,512]{1,0:T(8,128)(2,1)} fusion(bf16[1024,512]{1,0:T(8,128)(2,1)S(1)} %copy-done.1, bf16[1024,1024]{1,0:T(8,128)(2,1)S(1)} %shard_map.91, bf16[1024,512]{1,0:T(8,128)(2,1)S(1)} %copy-done), kind=kOutput, calls=%fused_computation | convolution fusion | flops 1075314688 | bytes 5242880 | tf_op jit(solution)/shard_map/dot_general | solution.py:441
Async XLA Ops:
  0.0 42.7 %copy-start = (bf16[1024,512]{1,0:T(8,128)(2,1)S(1)}, bf16[1024,512]{1,0:T(8,128)(2,1)}, u32[]{:S(2)}) copy-start(bf16[1024,512]{1,0:T(8,128)(2,1)} %param.17) | copy-start | bytes 3145732
  0.0 42.7 %copy-start.1 = (bf16[1024,512]{1,0:T(8,128)(2,1)S(1)}, bf16[1024,512]{1,0:T(8,128)(2,1)}, u32[]{:S(2)}) copy-start(bf16[1024,512]{1,0:T(8,128)(2,1)} %fine.1) | copy-start | bytes 3145732

commit v7 on v6

--- a/solution.py
+++ b/solution.py
@@ -202,6 +202,8 @@
         yslot[kk] = slots[kk : kk + 1, :]
     for data, slot in far_plane:
         data.wait_recv()
+    to_left.start()
+    to_right.start()
     zbuf[1, 0:16, :] = tbuf[1, pl.ds(pl.multiple_of(16 * xy, 16), 16), :]
     a = lax.broadcasted_iota(jnp.int32, (128, 128), 0)
     b = lax.broadcasted_iota(jnp.int32, (128, 128), 1)
@@ -221,8 +223,6 @@
         far_z[i][1].start()
     for i in (3, 4, 2, 5, 1, 6, 0, 7):
         far_z[i][0].start()
-    to_left.start()
-    to_right.start()
 
     lanes128 = lax.broadcasted_iota(jnp.int32, (1, 128), 1)
     lane_rows = lax.broadcasted_iota(jnp.int32, (WIN, 128), 1).astype(F32)

time: 45 us -> 39.7 us (0.88)
  the two profiles are of different devices: /device:TPU:1 before, /device:TPU:4 now
where the time goes in v7:
time: 39.7 us; the launch traced here: 39.6 us
  Pallas kernels  37.4 us (94%)
  matrix products  2.22 us (6%)
    pallas_call x1, Pallas kernels, on_device(): pl.pallas_call(kernel, out_shape=jax.ShapeDtypeStruct((rows, 2 * features...  37.4 us
    dot_general x1, matrix products, on_device(): branch = jnp.dot(joined, w_out, preferred_element_type=F32)  2.22 us

profile of v7, /device:TPU:4, one launch (start us, length us, event | category | flops | bytes accessed | tf_op | source)
XLA Modules:
  0.0 39.6 jit_solution(1324633941332582833)
XLA Ops:
  0.0 0.0 copy-start
  0.0 0.0 copy-start.1
  0.0 37.4 %shard_map.91 = bf16[1024,1024]{1,0:T(8,128)(2,1)S(1)} custom-call(bf16[1024,512]{1,0:T(8,128)(2,1)} %fine.1, bf16[256,512]{1,0:T(8,128)(2,1)} %par.1, s32[8,128]{1,0:T(8,128)} %bitcast.6, s32[2,1,128]{2,1,0:T(1,128)} %bitcast.9, f32[1,512]{1,0:T(1,128)} %bitcast.7, f32[1,512]{1,0:T(1,128)} %bitcast.8, bf16[512,1536]{1,0:T(8,128)(2,1)} %wqkv.1, ...), custom_call_target="tpu_custom_call" | custom-call | tf_op jit(solution)/shard_map/pallas_call | solution.py:377
  37.4 0.0 copy-done
  37.4 0.0 copy-done.1
  37.4 2.2 %add_convert_fusion = bf16[1024,512]{1,0:T(8,128)(2,1)} fusion(bf16[1024,512]{1,0:T(8,128)(2,1)S(1)} %copy-done.1, bf16[1024,1024]{1,0:T(8,128)(2,1)S(1)} %shard_map.91, bf16[1024,512]{1,0:T(8,128)(2,1)S(1)} %copy-done), kind=kOutput, calls=%fused_computation | convolution fusion | flops 1075314688 | bytes 5242880 | tf_op jit(solution)/shard_map/dot_general | solution.py:441
Async XLA Ops:
  0.0 37.4 %copy-start = (bf16[1024,512]{1,0:T(8,128)(2,1)S(1)}, bf16[1024,512]{1,0:T(8,128)(2,1)}, u32[]{:S(2)}) copy-start(bf16[1024,512]{1,0:T(8,128)(2,1)} %param.17) | copy-start | bytes 3145732
  0.0 37.4 %copy-start.1 = (bf16[1024,512]{1,0:T(8,128)(2,1)S(1)}, bf16[1024,512]{1,0:T(8,128)(2,1)}, u32[]{:S(2)}) copy-start(bf16[1024,512]{1,0:T(8,128)(2,1)} %fine.1) | copy-start | bytes 3145732

commit v8 on v7

--- a/solution.py
+++ b/solution.py
@@ -157,6 +157,15 @@
         far_plane[i][0].start()
         along_z[k][1].start()
         along_z[k][0].start()
+
+    @pl.when(xy == 0)
+    def _():
+        to_left.start()
+
+    @pl.when(xy == XYN - 1)
+    def _():
+        to_right.start()
+
     loads[4].wait()
     loads[5].wait()
     place = lax.broadcasted_iota(jnp.int32, (8, 128), 0) * 128 + lax.broadcasted_iota(
@@ -202,8 +211,15 @@
         yslot[kk] = slots[kk : kk + 1, :]
     for data, slot in far_plane:
         data.wait_recv()
-    to_left.start()
-    to_right.start()
+
+    @pl.when(xy != 0)
+    def _():
+        to_left.start()
+
+    @pl.when(xy != XYN - 1)
+    def _():
+        to_right.start()
+
     zbuf[1, 0:16, :] = tbuf[1, pl.ds(pl.multiple_of(16 * xy, 16), 16), :]
     a = lax.broadcasted_iota(jnp.int32, (128, 128), 0)
     b = lax.broadcasted_iota(jnp.int32, (128, 128), 1)

time: 39.7 us -> 39 us (0.982)
  Pallas kernels: 37.4 us -> 36.6 us
    pallas_call x1, Pallas kernels: 37.4 us -> 36.6 us  [on_device(): pl.pallas_call(kernel, out_shape=jax.ShapeDtypeStruct((rows, 2 * features...]
where the time goes in v8:
time: 39 us; the launch traced here: 38.9 us
  Pallas kernels  36.6 us (94%)
  matrix products  2.22 us (6%)
    pallas_call x1, Pallas kernels, on_device(): pl.pallas_call(kernel, out_shape=jax.ShapeDtypeStruct((rows, 2 * features...  36.6 us
    dot_general x1, matrix products, on_device(): branch = jnp.dot(joined, w_out, preferred_element_type=F32)  2.22 us

profile of v8, /device:TPU:4, one launch (start us, length us, event | category | flops | bytes accessed | tf_op | source)
XLA Modules:
  0.0 38.9 jit_solution(16525031058917697053)
XLA Ops:
  0.0 0.0 copy-start
  0.0 0.0 copy-start.1
  0.0 36.6 %shard_map.91 = bf16[1024,1024]{1,0:T(8,128)(2,1)S(1)} custom-call(bf16[1024,512]{1,0:T(8,128)(2,1)} %fine.1, bf16[256,512]{1,0:T(8,128)(2,1)} %par.1, s32[8,128]{1,0:T(8,128)} %bitcast.6, s32[2,1,128]{2,1,0:T(1,128)} %bitcast.9, f32[1,512]{1,0:T(1,128)} %bitcast.7, f32[1,512]{1,0:T(1,128)} %bitcast.8, bf16[512,1536]{1,0:T(8,128)(2,1)} %wqkv.1, ...), custom_call_target="tpu_custom_call" | custom-call | tf_op jit(solution)/shard_map/pallas_call | solution.py:393
  36.7 0.0 copy-done
  36.7 0.0 copy-done.1
  36.7 2.2 %add_convert_fusion = bf16[1024,512]{1,0:T(8,128)(2,1)} fusion(bf16[1024,512]{1,0:T(8,128)(2,1)S(1)} %copy-done.1, bf16[1024,1024]{1,0:T(8,128)(2,1)S(1)} %shard_map.91, bf16[1024,512]{1,0:T(8,128)(2,1)S(1)} %copy-done), kind=kOutput, calls=%fused_computation | convolution fusion | flops 1075314688 | bytes 5242880 | tf_op jit(solution)/shard_map/dot_general | solution.py:457
Async XLA Ops:
  0.0 36.7 %copy-start = (bf16[1024,512]{1,0:T(8,128)(2,1)S(1)}, bf16[1024,512]{1,0:T(8,128)(2,1)}, u32[]{:S(2)}) copy-start(bf16[1024,512]{1,0:T(8,128)(2,1)} %param.17) | copy-start | bytes 3145732
  0.0 36.7 %copy-start.1 = (bf16[1024,512]{1,0:T(8,128)(2,1)S(1)}, bf16[1024,512]{1,0:T(8,128)(2,1)}, u32[]{:S(2)}) copy-start(bf16[1024,512]{1,0:T(8,128)(2,1)} %fine.1) | copy-start | bytes 3145732

commit v9 on v8

--- a/solution.py
+++ b/solution.py
@@ -94,13 +94,6 @@
     peers += [left, right]
     for peer in peers:
         pl.semaphore_signal(barrier, inc=1, device_id={"pix": peer}, device_id_type=MESH)
-
-    a = lax.broadcasted_iota(jnp.int32, (128, 256), 0)
-    b = lax.broadcasted_iota(jnp.int32, (128, 256), 1)
-    chosen = 16 * ((z + FAR[0] + (a // 2) % 8) % ZN) + 2 * (a // 16) + a % 2
-    pick_far = (b == chosen).astype(F32).astype(BF16)
-    loads[9].wait()
-    tbuf[1] = dot(pick_far, parv[...]).astype(BF16)
 
     pl.semaphore_wait(barrier, len(peers))
     for k in (4, 12):
@@ -152,9 +145,8 @@
         )
         slot = remote(pslot, xslot.at[m], pss_sem.at[1, m], psr_sem.at[1, m], peer)
         far_plane.append((data, slot))
-    for i, k in enumerate((4, 12 + 1, 3, 14, 2, 15, 1)):
+    for i, k in enumerate((4, 13, 3, 14, 2, 15, 1)):
         far_plane[i][1].start()
-        far_plane[i][0].start()
         along_z[k][1].start()
         along_z[k][0].start()
 
@@ -165,6 +157,16 @@
     @pl.when(xy == XYN - 1)
     def _():
         to_right.start()
+
+    a = lax.broadcasted_iota(jnp.int32, (128, 256), 0)
+    b = lax.broadcasted_iota(jnp.int32, (128, 256), 1)
+    chosen = 16 * ((z + FAR[0] + (a // 2) % 8) % ZN) + 2 * (a // 16) + a % 2
+    pick_far = (b == chosen).astype(F32).astype(BF16)
+    loads[9].wait()
+    tbuf[1] = dot(pick_far, parv[...]).astype(BF16)
+    zbuf[1, 0:16, :] = tbuf[1, pl.ds(pl.multiple_of(16 * xy, 16), 16), :]
+    for data, slot in far_plane:
+        data.start()
 
     loads[4].wait()
     loads[5].wait()
@@ -220,7 +222,6 @@
     def _():
         to_right.start()
 
-    zbuf[1, 0:16, :] = tbuf[1, pl.ds(pl.multiple_of(16 * xy, 16), 16), :]
     a = lax.broadcasted_iota(jnp.int32, (128, 128), 0)
     b = lax.broadcasted_iota(jnp.int32, (128, 128), 1)
     order = (b == (a % 8) * 16 + (a // 16) * 2 + (a // 8) % 2).astype(F32).astype(BF16)

time: 39 us -> 39 us (level)
  no operation moved by 1% of the time
where the time goes in v9:
time: 39 us; the launch traced here: 38.9 us
  Pallas kernels  36.6 us (94%)
  matrix products  2.22 us (6%)
    pallas_call x1, Pallas kernels, on_device(): pl.pallas_call(kernel, out_shape=jax.ShapeDtypeStruct((rows, 2 * features...  36.6 us
    dot_general x1, matrix products, on_device(): branch = jnp.dot(joined, w_out, preferred_element_type=F32)  2.22 us

profile of v9, /device:TPU:4, one launch (start us, length us, event | category | flops | bytes accessed | tf_op | source)
XLA Modules:
  0.0 38.9 jit_solution(8170811926881895106)
XLA Ops:
  0.0 0.0 copy-start
  0.0 0.0 copy-start.1
  0.0 36.6 %shard_map.91 = bf16[1024,1024]{1,0:T(8,128)(2,1)S(1)} custom-call(bf16[1024,512]{1,0:T(8,128)(2,1)} %fine.1, bf16[256,512]{1,0:T(8,128)(2,1)} %par.1, s32[8,128]{1,0:T(8,128)} %bitcast.6, s32[2,1,128]{2,1,0:T(1,128)} %bitcast.9, f32[1,512]{1,0:T(1,128)} %bitcast.7, f32[1,512]{1,0:T(1,128)} %bitcast.8, bf16[512,1536]{1,0:T(8,128)(2,1)} %wqkv.1, ...), custom_call_target="tpu_custom_call" | custom-call | tf_op jit(solution)/shard_map/pallas_call | solution.py:394
  36.7 0.0 copy-done
  36.7 0.0 copy-done.1
  36.7 2.2 %add_convert_fusion = bf16[1024,512]{1,0:T(8,128)(2,1)} fusion(bf16[1024,512]{1,0:T(8,128)(2,1)S(1)} %copy-done.1, bf16[1024,1024]{1,0:T(8,128)(2,1)S(1)} %shard_map.91, bf16[1024,512]{1,0:T(8,128)(2,1)S(1)} %copy-done), kind=kOutput, calls=%fused_computation | convolution fusion | flops 1075314688 | bytes 5242880 | tf_op jit(solution)/shard_map/dot_general | solution.py:458
Async XLA Ops:
  0.0 36.7 %copy-start = (bf16[1024,512]{1,0:T(8,128)(2,1)S(1)}, bf16[1024,512]{1,0:T(8,128)(2,1)}, u32[]{:S(2)}) copy-start(bf16[1024,512]{1,0:T(8,128)(2,1)} %param.17) | copy-start | bytes 3145732
  0.0 36.7 %copy-start.1 = (bf16[1024,512]{1,0:T(8,128)(2,1)S(1)}, bf16[1024,512]{1,0:T(8,128)(2,1)}, u32[]{:S(2)}) copy-start(bf16[1024,512]{1,0:T(8,128)(2,1)} %fine.1) | copy-start | bytes 3145732

commit v10 on v9

--- a/solution.py
+++ b/solution.py
@@ -58,7 +58,7 @@
 def kernel(
     fine, par, shift, pslot, fgain, pgain, wqkv, wpar, out,
     xv, ext, halo, qv, kv, vt, ot, relb, shv, fgv, pgv,
-    wq, wp, wvt, zbuf, tbuf, fbuf, zslot, fslot, parv, xbuf, xslot, yslot, sslot, kpv, cot,
+    wq, wp, wvt, zbuf, tbuf, fbuf, zslot, fslot, parv, xbuf, xslot, yslot, sslot, kpv,
     s0, s1, s2, s3, p0, p1, p2, p3,
     in_sem, own_sem, hs_sem, hr_sem, zs_sem, zr_sem, zss_sem, zsr_sem,
     ps_sem, pr_sem, pss_sem, psr_sem, far_sem,
@@ -369,10 +369,9 @@
         w, at = u // groups, 128 * (u % groups)
         part = kpv[PWIN * w : PWIN * (w + 1), features + at : features + at + 128]
         stacked = jnp.concatenate([part * mask for mask in head_masks], axis=0)
-        cot[w, at : at + 128, :] = dot(stacked, weights, TN).astype(BF16)
-        if u % groups == groups - 1:
-            here = slice(WIN * w, WIN * (w + 1))
-            out[here, features:] = jnp.transpose(cot[w])
+        here = slice(WIN * w, WIN * (w + 1))
+        result = dot(stacked, weights, TN).astype(BF16)
+        out[here, features + at : features + at + 128] = jnp.transpose(result)
 
     staged(windows * groups, PWIN, cross_scores, cross_values, sbufs, pbufs)
 
@@ -422,7 +421,6 @@
             vmem((8, 1, 128), F32),
             vmem((8, 1, 128), F32),
             vmem((256, 2 * features), BF16),
-            vmem((4, features, WIN), BF16),
             *[vmem((WIN, WIN), F32)] * 4,
             *[vmem((WIN, WIN), BF16)] * 4,
             dma((10,)),

time: 39 us -> 39 us (level)
  no operation moved by 1% of the time
where the time goes in v10:
time: 39 us; the launch traced here: 38.9 us
  Pallas kernels  36.7 us (94%)
  matrix products  2.22 us (6%)
    pallas_call x1, Pallas kernels, on_device(): pl.pallas_call(kernel, out_shape=jax.ShapeDtypeStruct((rows, 2 * features...  36.7 us
    dot_general x1, matrix products, on_device(): branch = jnp.dot(joined, w_out, preferred_element_type=F32)  2.22 us

profile of v10, /device:TPU:4, one launch (start us, length us, event | category | flops | bytes accessed | tf_op | source)
XLA Modules:
  0.0 38.9 jit_solution(12542629912409224578)
XLA Ops:
  0.0 0.0 copy-start
  0.0 0.0 copy-start.1
  0.0 36.7 %shard_map.91 = bf16[1024,1024]{1,0:T(8,128)(2,1)S(1)} custom-call(bf16[1024,512]{1,0:T(8,128)(2,1)} %fine.1, bf16[256,512]{1,0:T(8,128)(2,1)} %par.1, s32[8,128]{1,0:T(8,128)} %bitcast.6, s32[2,1,128]{2,1,0:T(1,128)} %bitcast.9, f32[1,512]{1,0:T(1,128)} %bitcast.7, f32[1,512]{1,0:T(1,128)} %bitcast.8, bf16[512,1536]{1,0:T(8,128)(2,1)} %wqkv.1, ...), custom_call_target="tpu_custom_call" | custom-call | tf_op jit(solution)/shard_map/pallas_call | solution.py:393
  36.7 0.0 copy-done
  36.7 0.0 copy-done.1
  36.7 2.2 %add_convert_fusion = bf16[1024,512]{1,0:T(8,128)(2,1)} fusion(bf16[1024,512]{1,0:T(8,128)(2,1)S(1)} %copy-done.1, bf16[1024,1024]{1,0:T(8,128)(2,1)S(1)} %shard_map.91, bf16[1024,512]{1,0:T(8,128)(2,1)S(1)} %copy-done), kind=kOutput, calls=%fused_computation | convolution fusion | flops 1075314688 | bytes 5242880 | tf_op jit(solution)/shard_map/dot_general | solution.py:456
Async XLA Ops:
  0.0 36.7 %copy-start = (bf16[1024,512]{1,0:T(8,128)(2,1)S(1)}, bf16[1024,512]{1,0:T(8,128)(2,1)}, u32[]{:S(2)}) copy-start(bf16[1024,512]{1,0:T(8,128)(2,1)} %param.17) | copy-start | bytes 3145732
  0.0 36.7 %copy-start.1 = (bf16[1024,512]{1,0:T(8,128)(2,1)S(1)}, bf16[1024,512]{1,0:T(8,128)(2,1)}, u32[]{:S(2)}) copy-start(bf16[1024,512]{1,0:T(8,128)(2,1)} %fine.1) | copy-start | bytes 3145732
